TPU v7x, 512 devices: a whole 4x8x8 slice. The times are simulated.
512 devices in a mesh: dp: 32 (over y, x), seq: 16 (over z, core).
Axes of the slice: x: 4, y: 8, z: 8, core: 2. Of those that a mesh axis runs over, the one named last changes fastest.
Arguments:
- queries: bfloat16 [32, 2048, 3072], P('dp', 'seq'), may hold values from -6 to 6
- key_states: bfloat16 [32, 2048, 3072], P('dp', 'seq'), may hold values from -6 to 6
- value_states: bfloat16 [32, 2048, 3072], P('dp', 'seq'), may hold values from -6 to 6
- cotangent: bfloat16 [32, 2048, 128], P('dp', 'seq'), may hold values from -6 to 6
- norm_gains: float32 [2, 128], P(None, 'dp'), may hold values from 0.5 to 1.5
- tile_lists: int32 [32, 4], replicated, may hold values from -1 to 31, as said below
- clip_lengths: int32 [32], P('dp'), may hold values from 1024 to 2048
Outputs:
- query_grad: bfloat16 [32, 2048, 3072], P('dp', 'seq')
- key_grad: bfloat16 [32, 2048, 3072], P('dp', 'seq')
- value_grad: bfloat16 [32, 2048, 3072], P('dp', 'seq')
- gain_grad: float32 [2, 128], P(None, 'dp')
Inputs may be any that keep to these rules, and one draw needn't show every extreme that they name: `tile_lists`: row i names tile 0 in its first slot; for i > 0 its second slot names tile i; the other names of a row are distinct tiles other than 0; between 3 and 4 slots of a row name tiles and the rest are -1; row 0 has at least one -1.
All inputs are finite; a program needn't handle non-finite values.
Results may differ from a plain program's by a relative error of at most 0.0086.
Values may be sent and summed in bfloat16 or wider, within the bound.
A program may use at most 128 MiB of HBM per device.

v0:
```python
import math

import jax
import jax.numpy as jnp
from jax import lax
from jax.sharding import PartitionSpec as P

HEAD_DIM = 128
TILE = 64


EPS = 1e-06


def rms_parts(raw_rows, gain_row, head_count):
    widened = raw_rows.astype(jnp.float32).reshape(raw_rows.shape[0], head_count, HEAD_DIM)
    inverse = lax.rsqrt(jnp.mean(widened * widened, axis=-1, keepdims=True) + EPS)
    return (widened, inverse, (widened * inverse * gain_row).astype(jnp.bfloat16))


def rms_back(widened, inverse, gain_row, upstream):
    incoming = upstream.astype(jnp.float32)
    scaled = incoming * gain_row
    inner_sum = jnp.mean(widened * scaled, axis=-1, keepdims=True)
    grad_rows = inverse * scaled - widened * inverse * inverse * inverse * inner_sum
    return (grad_rows, jnp.sum(incoming * widened * inverse, axis=(0, 1)))


def parity_layout(row_data, group_count, half_count):
    token_count = row_data.shape[0]
    feature = row_data.shape[1] // group_count
    shaped = row_data.reshape(
        token_count // (TILE * half_count), half_count, TILE, group_count, feature
    )
    return shaped.transpose(3, 1, 0, 2, 4).reshape(group_count * half_count, -1, feature)


def parity_restore(pieces, group_count, half_count):
    feature = pieces.shape[-1]
    shaped = pieces.reshape(group_count, half_count, -1, TILE, feature)
    return shaped.transpose(2, 1, 3, 0, 4).reshape(-1, group_count * feature)


def copies_layout(row_data, group_count, half_count):
    token_count = row_data.shape[0]
    feature = row_data.shape[1] // group_count
    shaped = row_data.reshape(token_count, group_count, feature).transpose(1, 0, 2)
    spread_rows = jnp.broadcast_to(shaped[:, None], (group_count, half_count, token_count, feature))
    return spread_rows.reshape(group_count * half_count, token_count, feature)


def shared_layout(row_data, group_count, half_count):
    token_count = row_data.shape[0]
    feature = row_data.shape[1]
    shaped = row_data.reshape(
        token_count // (TILE * half_count), half_count, TILE, feature
    ).transpose(1, 0, 2, 3)
    spread_rows = jnp.broadcast_to(shaped[None], (group_count,) + shaped.shape)
    return spread_rows.reshape(group_count * half_count, -1, feature)


def block_grads(query_tiles, cot_tiles, list_block, key_tiles, value_tiles, length):
    factor = 1.0 / math.sqrt(HEAD_DIM)
    tiles_here = list_block.shape[0]
    slot_count = list_block.shape[1]
    local_heads = key_tiles.shape[1]
    merged = slot_count * TILE
    safe_ids = jnp.maximum(list_block, 0)
    key_rows = (
        key_tiles[safe_ids]
        .transpose(0, 2, 1, 3, 4)
        .reshape(tiles_here, local_heads, merged, HEAD_DIM)
    )
    value_rows = (
        value_tiles[safe_ids]
        .transpose(0, 2, 1, 3, 4)
        .reshape(tiles_here, local_heads, merged, HEAD_DIM)
    )
    positions = safe_ids[:, :, None] * TILE + jnp.arange(TILE, dtype=jnp.int32)[None, None, :]
    usable = (
        jnp.logical_and(list_block[:, :, None] >= 0, positions < length)
        .astype(jnp.float32)
        .reshape(tiles_here, merged)
    )
    scores = (
        jnp.einsum("ghqd,ghmd->ghqm", query_tiles, key_rows, preferred_element_type=jnp.float32)
        * factor
    )
    weights = jnp.exp(scores) * usable[:, None, None, :]
    prob_rows = weights / jnp.sum(weights, axis=3, keepdims=True)
    prob_low = prob_rows.astype(jnp.bfloat16)
    attended = jnp.einsum(
        "ghqm,ghmd->ghqd", prob_low, value_rows, preferred_element_type=jnp.float32
    )
    diag_term = jnp.sum(cot_tiles.astype(jnp.float32)[:, None, :, :] * attended, axis=-1)
    grad_probs = jnp.einsum(
        "gqd,ghmd->ghqm", cot_tiles, value_rows, preferred_element_type=jnp.float32
    )
    grad_low = (prob_rows * (grad_probs - diag_term[:, :, :, None])).astype(jnp.bfloat16)
    grad_query = (
        jnp.einsum("ghqm,ghmd->ghqd", grad_low, key_rows, preferred_element_type=jnp.float32)
        * factor
    ).astype(jnp.bfloat16)
    grad_keys = (
        jnp.einsum("ghqm,ghqd->ghmd", grad_low, query_tiles, preferred_element_type=jnp.float32)
        * factor
    )
    grad_values = jnp.einsum(
        "ghqm,gqd->ghmd", prob_low, cot_tiles, preferred_element_type=jnp.float32
    )
    grad_keys = grad_keys.reshape(tiles_here, local_heads, slot_count, TILE, HEAD_DIM).transpose(
        0, 2, 1, 3, 4
    )
    grad_values = grad_values.reshape(
        tiles_here, local_heads, slot_count, TILE, HEAD_DIM
    ).transpose(0, 2, 1, 3, 4)
    return (safe_ids.reshape(-1), grad_query, grad_keys, grad_values)


def body(queries, key_states, value_states, cotangent, norm_gains, tile_lists, clip_lengths):
    seq_count = lax.axis_size("seq")
    seq_index = lax.axis_index("seq")
    token_count = queries.shape[1]
    head_count = queries.shape[2] // HEAD_DIM
    group_count = math.gcd(head_count, seq_count)
    half_count = seq_count // group_count
    local_heads = head_count // group_count
    feature = local_heads * HEAD_DIM
    tile_count = token_count * seq_count // TILE
    mine_count = tile_count // half_count
    slot_count = tile_lists.shape[1]
    parity = seq_index % half_count
    length = clip_lengths[0]
    gain_rows = lax.all_gather(norm_gains, "dp", axis=1, tiled=True)
    query_wide, query_inv, query_norm = rms_parts(queries[0], gain_rows[0], head_count)
    keys_wide, keys_inv, keys_norm = rms_parts(key_states[0], gain_rows[1], head_count)
    positions = seq_index * token_count + jnp.arange(token_count, dtype=jnp.int32)
    cot_live = jnp.where((positions < length)[:, None], cotangent[0], jnp.zeros_like(cotangent[0]))
    send_query = parity_layout(query_norm.reshape(token_count, -1), group_count, half_count)
    send_cot = shared_layout(cot_live, group_count, half_count)
    keys_flat = keys_norm.reshape(token_count, -1)
    got_query, got_cot, got_keys, got_values = (
        lax.all_to_all(send_query, "seq", split_axis=0, concat_axis=0, tiled=True),
        lax.all_to_all(send_cot, "seq", split_axis=0, concat_axis=0, tiled=True),
        lax.all_to_all(
            copies_layout(keys_flat, group_count, half_count),
            "seq",
            split_axis=0,
            concat_axis=0,
            tiled=True,
        ),
        lax.all_to_all(
            copies_layout(value_states[0], group_count, half_count),
            "seq",
            split_axis=0,
            concat_axis=0,
            tiled=True,
        ),
    )
    key_arranged = got_keys.reshape(tile_count, TILE, local_heads, HEAD_DIM)
    value_arranged = got_values.reshape(tile_count, TILE, local_heads, HEAD_DIM)
    key_tiles = key_arranged.transpose(0, 2, 1, 3)
    value_tiles = value_arranged.transpose(0, 2, 1, 3)
    query_tiles = got_query.reshape(mine_count, TILE, local_heads, HEAD_DIM).transpose(0, 2, 1, 3)
    my_lists = lax.dynamic_slice_in_dim(
        tile_lists.reshape(mine_count, half_count * slot_count), parity * slot_count, slot_count, 1
    )
    block_size = math.gcd(mine_count, 8)
    block_count = mine_count // block_size

    def tile_step(carried, inputs):
        acc_keys, acc_values = carried
        query_block, cot_block, list_block = inputs
        where_rows, grad_query, grad_keys, grad_values = block_grads(
            query_block, cot_block, list_block, key_tiles, value_tiles, length
        )
        acc_keys = acc_keys.at[where_rows].add(grad_keys.reshape(-1, local_heads, TILE, HEAD_DIM))
        acc_values = acc_values.at[where_rows].add(
            grad_values.reshape(-1, local_heads, TILE, HEAD_DIM)
        )
        return ((acc_keys, acc_values), grad_query)

    empty_acc = jnp.zeros((tile_count, local_heads, TILE, HEAD_DIM), jnp.float32)
    scanned = (
        query_tiles.reshape(block_count, block_size, local_heads, TILE, HEAD_DIM),
        got_cot.reshape(block_count, block_size, TILE, HEAD_DIM),
        my_lists.reshape(block_count, block_size, slot_count),
    )
    (acc_keys, acc_values), grad_query = lax.scan(tile_step, (empty_acc, empty_acc), scanned)
    query_rows_back = grad_query.reshape(mine_count, local_heads, TILE, HEAD_DIM).transpose(
        0, 2, 1, 3
    )
    back_query = lax.all_to_all(
        query_rows_back.reshape(seq_count, -1, feature),
        "seq",
        split_axis=0,
        concat_axis=0,
        tiled=True,
    )
    query_grad_norm = parity_restore(back_query, group_count, half_count)
    stacked = jnp.stack([acc_keys, acc_values], 0).transpose(0, 1, 3, 2, 4)
    stacked = stacked.reshape(2, tile_count, TILE, feature).astype(jnp.bfloat16)
    pieces = lax.all_to_all(
        stacked.reshape(2, seq_count, token_count, feature),
        "seq",
        split_axis=1,
        concat_axis=1,
        tiled=True,
    )
    summed = jnp.sum(
        pieces.astype(jnp.float32).reshape(2, group_count, half_count, token_count, feature), axis=2
    )
    grads_low = summed.transpose(0, 2, 1, 3).reshape(2, token_count, -1).astype(jnp.bfloat16)
    query_grad, gain_query = rms_back(
        query_wide,
        query_inv,
        gain_rows[0],
        query_grad_norm.reshape(token_count, head_count, HEAD_DIM),
    )
    key_grad, gain_keys = rms_back(
        keys_wide, keys_inv, gain_rows[1], grads_low[0].reshape(token_count, head_count, HEAD_DIM)
    )
    gain_terms = jnp.stack([gain_query, gain_keys], 0)
    norm_factor = 1.0 / math.sqrt(lax.axis_size("dp") * token_count * seq_count * head_count)
    over_seq = lax.psum(gain_terms, "seq")
    gain_grad = lax.psum_scatter(over_seq, "dp", scatter_dimension=1, tiled=True)
    return (
        query_grad.reshape(1, token_count, -1).astype(jnp.bfloat16),
        key_grad.reshape(1, token_count, -1).astype(jnp.bfloat16),
        grads_low[1][None],
        gain_grad * norm_factor,
    )


def solution(mesh):
    placed = (
        P("dp", "seq", None),
        P("dp", "seq", None),
        P("dp", "seq", None),
        P("dp", "seq", None),
        P(None, "dp"),
        P(),
        P("dp"),
    )
    return jax.shard_map(
        body,
        mesh=mesh,
        in_specs=placed,
        out_specs=(P("dp", "seq", None), P("dp", "seq", None), P("dp", "seq", None), P(None, "dp")),
        check_vma=False,
    )
```

profile of v0, /device:TPU:1, one launch (start us, length us, event | category | flops | bytes accessed | tf_op | source)
XLA Modules:
  0.0 481.5 jit_solution(13979049925993174147)
XLA Ops:
  0.6 32.2 %all-gather = f32[32,4,2]{1,2,0:T(2,128)S(1)} all-gather(f32[1,4,2]{1,2,0:T(2,128)} %bitcast.247), channel_id=1, replica_groups=mesh['dp'=32,'seq'=16] {'dp'}, dimensions={0}, use_global_device_ids=true | all-gather | bytes 1056 | tf_op jit(solution)/shard_map/all_gather | solution.py:134
  33.0 1.3 convert_bitcast_fusion.2
  34.7 1.4 copy-done.6
  36.8 1.7 mul.311
  38.5 1.6 mul.314
  42.3 19.1 %all-to-all-start = ((bf16[16,64,384]{2,1,0:T(8,128)(2,1)}), bf16[16,64,384]{2,1,0:T(8,128)(2,1)S(1)}, u32[]{:S(2)}, u32[]{:S(2)}) async-start(bf16[16,64,384]{2,1,0:T(8,128)(2,1)} %bitcast.24), calls=%async_computation | async-start | bytes 1572864 | tf_op jit(solution)/shard_map/all_to_all | solution.py:143
  61.6 22.4 %all-to-all-done = bf16[16,64,384]{2,1,0:T(8,128)(2,1)S(1)} async-done(((bf16[16,64,384]{2,1,0:T(8,128)(2,1)}), bf16[16,64,384]{2,1,0:T(8,128)(2,1)S(1)}, u32[]{:S(2)}, u32[]{:S(2)}) %all-to-all-start) | async-done | bytes 786464 | tf_op jit(solution)/shard_map/all_to_all | solution.py:143
  84.0 1.4 broadcast_in_dim.28
  85.4 3.6 all-to-all-start.2
  89.0 1.5 copy.202
  93.5 33.5 %all-to-all-done.2 = bf16[16,128,384]{2,1,0:T(8,128)(2,1)S(1)} async-done(((bf16[16,128,384]{2,1,0:T(8,128)(2,1)}), bf16[16,128,384]{2,1,0:T(8,128)(2,1)S(1)}, u32[]{:S(2)}, u32[]{:S(2)}) %all-to-all-start.2) | async-done | bytes 1572896 | tf_op jit(solution)/shard_map/all_to_all | solution.py:152
  127.0 3.0 broadcast_in_dim.27
  130.1 4.4 all-to-all-start.1
  135.3 37.7 %all-to-all-done.1 = bf16[16,128,384]{2,1,0:T(8,128)(2,1)} async-done(((bf16[16,128,384]{2,1,0:T(8,128)(2,1)}), bf16[16,128,384]{2,1,0:T(8,128)(2,1)}, u32[]{:S(2)}, u32[]{:S(2)}) %all-to-all-start.1) | async-done | bytes 1572896 | tf_op jit(solution)/shard_map/all_to_all | solution.py:145
  173.8 4.3 all-to-all-start.3
  179.8 3.9 reshape.376
  183.7 1.6 copy.208
  185.2 3.9 reshape.374
  189.2 1.6 copy.207
  190.7 2.1 broadcast_in_dim.25.clone
  192.8 2.1 broadcast_in_dim.25
  194.9 67.8 %while.14 = (s32[]{:T(128)}, f32[32,3,64,128]{3,2,1,0:T(8,128)}, f32[32,3,64,128]{3,2,1,0:T(8,128)}, bf16[2,8,3,64,128]{4,3,2,1,0:T(8,128)(2,1)}, s32[2,8,4]{1,2...) while((s32[]{:T(128)}, f32[32,3,64,128]{3,2,1,0:T(8,128)}, ...), condition=%wide.region_7.8_spmd, body=%wide.region_2.7_spmd.sunk | while | flops 615064960 | bytes 89471312 | solution.py:189
  197.3 2.3 gather_fusion.1
  199.7 2.3 gather_fusion
  202.0 1.4 copy.243
  203.4 2.3 fusion.79
  206.2 1.7 fusion.81
  210.0 1.5 fusion.83
  212.0 7.3 %scatter_fusion.1 = f32[32,3,64,128]{3,2,1,0:T(8,128)} fusion(f32[32,3,64,128]{3,2,1,0:T(8,128)} %get-tuple-element.303, s32[32]{0:T(128)S(1)} %reshape.454, f32[32,3,64,128]{3,2,1,0:T(8,128)S(1)} %bitcast.216), kind=kCustom, calls=%fused_computation.3.clone.1 | custom fusion | flops 786432 | bytes 9437312 | tf_op jit(solution)/shard_map/while/body/eval_jaxpr/scatter-add | solution.py:178
  219.3 1.8 convolution_multiply_fusion.4
  221.6 7.1 %scatter_fusion = f32[32,3,64,128]{3,2,1,0:T(8,128)} fusion(f32[32,3,64,128]{3,2,1,0:T(8,128)} %get-tuple-element.302, s32[32]{0:T(128)S(1)} %reshape.454, f32[32,3,64,128]{3,2,1,0:T(8,128)S(1)} %bitcast.215), kind=kCustom, calls=%fused_computation.2.clone.1 | custom fusion | flops 786432 | bytes 9437312 | tf_op jit(solution)/shard_map/while/body/eval_jaxpr/scatter-add | solution.py:177
  231.0 2.3 gather_fusion.1
  233.5 2.3 gather_fusion
  235.8 1.4 copy.243
  237.1 2.3 fusion.79
  240.0 1.7 fusion.81
  243.7 1.5 fusion.83
  245.7 7.6 %scatter_fusion.1 = f32[32,3,64,128]{3,2,1,0:T(8,128)} fusion(f32[32,3,64,128]{3,2,1,0:T(8,128)} %get-tuple-element.303, s32[32]{0:T(128)S(1)} %reshape.454, f32[32,3,64,128]{3,2,1,0:T(8,128)S(1)} %bitcast.216), kind=kCustom, calls=%fused_computation.3.clone.1 | custom fusion | flops 786432 | bytes 9437312 | tf_op jit(solution)/shard_map/while/body/eval_jaxpr/scatter-add | solution.py:178
  253.3 1.8 convolution_multiply_fusion.4
  255.6 7.0 %scatter_fusion = f32[32,3,64,128]{3,2,1,0:T(8,128)} fusion(f32[32,3,64,128]{3,2,1,0:T(8,128)} %get-tuple-element.302, s32[32]{0:T(128)S(1)} %reshape.454, f32[32,3,64,128]{3,2,1,0:T(8,128)S(1)} %bitcast.215), kind=kCustom, calls=%fused_computation.2.clone.1 | custom fusion | flops 786432 | bytes 9437312 | tf_op jit(solution)/shard_map/while/body/eval_jaxpr/scatter-add | solution.py:177
  262.7 2.8 copy.236
  265.4 3.4 reshape.379
  268.8 7.2 %all-to-all-start.4 = ((bf16[16,64,384]{2,1,0:T(8,128)(2,1)}), bf16[16,64,384]{2,1,0:T(8,128)(2,1)}, u32[]{:S(2)}, u32[]{:S(2)}) async-start(bf16[16,64,384]{2,1,0:T(8,128)(2,1)} %reshape.379), calls=%async_computation.4 | async-start | bytes 1572864 | tf_op jit(solution)/shard_map/all_to_all | solution.py:193
  276.4 1.5 copy-done.2
  278.6 5.0 %copy.213 = bf16[2,32,64,3,128]{4,3,2,1,0:T(4,128)(2,1)} copy(bf16[2,32,64,3,128]{4,2,3,1,0:T(8,128)(2,1)S(1)} %maximum_bitcast_fusion) | data formatting | bytes 6291456 | tf_op jit(solution)/shard_map/convert_element_type | solution.py:202
  283.6 7.7 %convert_element_type.198 = bf16[2,16,128,384]{3,2,1,0:T(8,128)(2,1)S(1)} reshape(bf16[2,32,64,3,128]{4,3,2,1,0:T(4,128)(2,1)} %copy.213) | data formatting | bytes 6291456 | tf_op jit(solution)/shard_map/convert_element_type | solution.py:202
  291.3 2.1 copy.214
  293.4 5.5 %all-to-all-done.4 = bf16[16,64,384]{2,1,0:T(8,128)(2,1)} async-done(((bf16[16,64,384]{2,1,0:T(8,128)(2,1)}), bf16[16,64,384]{2,1,0:T(8,128)(2,1)}, u32[]{:S(2)}, u32[]{:S(2)}) %all-to-all-start.4) | async-done | bytes 786464 | tf_op jit(solution)/shard_map/all_to_all | solution.py:193
  298.8 4.4 all-to-all-start.5
  303.2 1.4 mul.312
  304.7 1.3 dynamic-slice
  306.6 1.3 bitcast_convert_fusion.1
  309.1 1.3 reshape.387
  310.3 1.4 reshape.386
  312.3 2.9 multiply_reduce_fusion
  315.3 1.9 multiply_reduce_fusion.2
  317.8 1.5 mul.343
  319.3 3.8 fusion.26
  323.1 50.0 %all-to-all-done.5 = bf16[2,16,128,384]{3,2,0,1:T(8,128)(2,1)} async-done(((bf16[2,16,128,384]{3,2,0,1:T(8,128)(2,1)}), bf16[2,16,128,384]{3,2,0,1:T(8,128)(2,1)}, u32[]{:S(2)}, u32[]{:S(2)}) %all-to-all-start.5) | async-done | bytes 3145760 | tf_op jit(solution)/shard_map/all_to_all | solution.py:203
  373.1 2.5 bitcast_reduce_fusion
  375.7 1.4 fusion.37
  378.3 2.0 copy.216
  382.4 58.3 %all-reduce = f32[2,128]{1,0:T(2,128)S(1)} all-reduce(f32[2,128]{1,0:T(2,128)S(1)} %pad_maximum_fusion.2), channel_id=2, replica_groups=mesh['dp'=32,'seq'=16] {'dp'}, use_global_device_ids=true, to_apply=%region_16.17.clone | all-reduce | flops 256 | bytes 2048
  441.9 37.8 %psum.8 = f32[2,4]{1,0:T(2,128)S(1)} all-reduce(f32[2,4]{1,0:T(2,128)S(1)} %constant_dynamic-slice_fusion), channel_id=1, replica_groups=mesh['dp'=32,'seq'=16] {'seq'}, use_global_device_ids=true, to_apply=%region_15.16 | all-reduce | flops 8 | bytes 64 | tf_op jit(solution)/shard_map/psum | solution.py:225
  (148 shorter events, 30.9 us)
Async XLA Ops:
  0.6 33.6 %copy-start.15 = (bf16[1,128,3072]{2,1,0:T(8,128)(2,1)S(1)}, bf16[1,128,3072]{2,1,0:T(8,128)(2,1)}, u32[]{:S(2)}) copy-start(bf16[1,128,3072]{2,1,0:T(8,128)(2,1)} %param.9) | copy-start | bytes 2359300
  34.4 5.7 %copy-start.8 = (f32[16,8,8,384]{3,2,1,0:T(8,128)}, f32[16,8,8,384]{3,2,1,0:T(8,128)S(1)}, u32[]{:S(2)}) copy-start(f32[16,8,8,384]{3,2,1,0:T(8,128)S(1)} %copy.227) | copy-start | bytes 4718596
  34.7 1.4 copy-start.6
  40.1 1.1 copy-start.10
  41.3 20.1 %copy-start.19 = (bf16[1,128,3072]{2,1,0:T(8,128)(2,1)S(1)}, bf16[1,128,3072]{2,1,0:T(8,128)(2,1)}, u32[]{:S(2)}) copy-start(bf16[1,128,3072]{2,1,0:T(8,128)(2,1)} %param.11) | copy-start | bytes 2359300
  42.3 41.8 %all-to-all-start = ((bf16[16,64,384]{2,1,0:T(8,128)(2,1)}), bf16[16,64,384]{2,1,0:T(8,128)(2,1)S(1)}, u32[]{:S(2)}, u32[]{:S(2)}) async-start(bf16[16,64,384]{2,1,0:T(8,128)(2,1)} %bitcast.24), calls=%async_computation | async-start | bytes 1572864 | tf_op jit(solution)/shard_map/all_to_all | solution.py:143
  85.4 41.6 %all-to-all-start.2 = ((bf16[16,128,384]{2,1,0:T(8,128)(2,1)}), bf16[16,128,384]{2,1,0:T(8,128)(2,1)S(1)}, u32[]{:S(2)}, u32[]{:S(2)}) async-start(bf16[16,128,384]{2,1,0:T(8,128)(2,1)} %bitcast.235), calls=%async_computation.2 | async-start | bytes 3145728 | tf_op jit(solution)/shard_map/all_to_all | solution.py:152
  90.6 0.9 copy-start.13
  90.7 1.4 copy-start.4
  91.5 0.6 copy-start.20
  127.0 3.0 copy-start.17
  130.1 5.1 %copy-start.22 = (bf16[1,128,128]{2,1,0:T(8,128)(2,1)S(1)}, bf16[1,128,128]{2,1,0:T(8,128)(2,1)}, u32[]{:S(2)}) copy-start(bf16[1,128,128]{2,1,0:T(8,128)(2,1)} %param.12) | copy-start | bytes 98308
  130.1 48.0 %copy-start.23 = (s32[32,4]{0,1:T(4,128)S(1)}, s32[32,4]{0,1:T(4,128)}, u32[]{:S(2)}) copy-start(s32[32,4]{0,1:T(4,128)} %param.14) | copy-start | bytes 1540
  130.1 42.9 %all-to-all-start.1 = ((bf16[16,128,384]{2,1,0:T(8,128)(2,1)}), bf16[16,128,384]{2,1,0:T(8,128)(2,1)}, u32[]{:S(2)}, u32[]{:S(2)}) async-start(bf16[16,128,384]{2,1,0:T(8,128)(2,1)} %bitcast.234), calls=%async_computation.1 | async-start | bytes 3145728 | tf_op jit(solution)/shard_map/all_to_all | solution.py:145
  173.8 17.0 %all-to-all-start.3 = ((bf16[16,64,128]{2,1,0:T(8,128)(2,1)}), bf16[16,64,128]{2,1,0:T(8,128)(2,1)}, u32[]{:S(2)}, u32[]{:S(2)}) async-start(bf16[16,64,128]{2,1,0:T(8,128)(2,1)} %bitcast.40), calls=%async_computation.3 | async-start | bytes 524288 | tf_op jit(solution)/shard_map/all_to_all | solution.py:144
  206.2 2.6 copy-start.1
  207.9 0.9 copy-start
  239.9 2.6 copy-start.1
  241.7 0.9 copy-start
  265.4 10.6 %copy-start.3 = (f32[32,3,64,128]{3,2,1,0:T(8,128)S(1)}, f32[32,3,64,128]{3,2,1,0:T(8,128)}, u32[]{:S(2)}) copy-start(f32[32,3,64,128]{3,2,1,0:T(8,128)} %get-tuple-element.59) | copy-start | bytes 9437188
  268.8 30.0 %all-to-all-start.4 = ((bf16[16,64,384]{2,1,0:T(8,128)(2,1)}), bf16[16,64,384]{2,1,0:T(8,128)(2,1)}, u32[]{:S(2)}, u32[]{:S(2)}) async-start(bf16[16,64,384]{2,1,0:T(8,128)(2,1)} %reshape.379), calls=%async_computation.4 | async-start | bytes 1572864 | tf_op jit(solution)/shard_map/all_to_all | solution.py:193
  276.0 1.9 copy-start.2
  293.3 9.9 %copy-start.11 = (f32[128,24,128]{2,1,0:T(8,128)S(1)}, f32[128,24,128]{2,1,0:T(8,128)}, u32[]{:S(2)}) copy-start(f32[128,24,128]{2,1,0:T(8,128)} %mul.311) | copy-start | bytes 4718596
  298.8 74.3 %all-to-all-start.5 = ((bf16[2,16,128,384]{3,2,0,1:T(8,128)(2,1)}), bf16[2,16,128,384]{3,2,0,1:T(8,128)(2,1)}, u32[]{:S(2)}, u32[]{:S(2)}) async-start(bf16[2,16,128,384]{3,2,0,1:T(8,128)(2,1)} %copy.214), calls=%async_computation.5 | async-start | bytes 6291456 | tf_op jit(solution)/shard_map/all_to_all | solution.py:203
  307.9 1.2 copy-start.12
  310.3 2.0 copy-start.9
  312.3 3.0 copy-start.7
  317.8 1.5 copy-start.16
  378.3 2.0 copy-start.5
  380.3 1.1 copy-start.14
  380.3 1.1 copy-start.21
  381.4 59.4 %copy-start.18 = (bf16[1,128,8,384]{1,3,2,0:T(8,128)(2,1)S(1)}, bf16[1,128,8,384]{1,3,2,0:T(8,128)(2,1)}, u32[]{:S(2)}) copy-start(bf16[1,128,8,384]{1,3,2,0:T(8,128)(2,1)} %copy.218) | copy-start | bytes 2359300
where the time goes:
time: 484 us; the launch traced here: 481 us
  waiting for transfers between devices  149 us (31%)
  blocking collectives  128 us (26%)
  local copies, waits for them, and re-layouts  87.9 us (18%)
  other arithmetic  52.3 us (11%)
  starting transfers between devices  43 us (9%)
  matrix products  18.2 us (4%)
    unnamed x1, blocking collectives  58.3 us
    all_to_all x1, waiting for transfers between devices, body(): lax.all_to_all(stacked.reshape(2, seq_count, token_count, feature), 'seq'...  50 us
    psum x1, blocking collectives, body(): over_seq = lax.psum(gain_terms, 'seq')  37.8 us
    all_to_all x1, waiting for transfers between devices, body(): lax.all_to_all(copies_layout(keys_flat, group_count, half_count), 'seq',...  37.7 us
    all_to_all x1, waiting for transfers between devices, body(): lax.all_to_all(copies_layout(value_states[0], group_count, half_count), '...  33.5 us
    all_gather x1, blocking collectives, body(): gain_rows = lax.all_gather(norm_gains, 'dp', axis=1, tiled=True)  32.2 us
    all_to_all x1, waiting for transfers between devices, body(): lax.all_to_all(send_query, 'seq', split_axis=0, concat_axis=0, tiled=True)  22.4 us
    all_to_all x1, starting transfers between devices, body(): lax.all_to_all(send_query, 'seq', split_axis=0, concat_axis=0, tiled=True)  19.1 us
  transfers between devices with their start and end apart: 6, of which 5 were waited for; matrix products, arithmetic and copies ran while one was open for 10% of the time, Pallas kernels for 0%

commit v1 on v0

v1 whole, which is shorter than its diff:
```python
import functools
import math


import jax
import jax.numpy as jnp
from jax import lax
from jax.experimental import pallas as pl
from jax.experimental.pallas import tpu as pltpu
import ml_dtypes
from jax.sharding import PartitionSpec as P

HEAD_DIM = 128
TILE = 64
EPS = 1e-06
BLOCK = 256
COLS = 4
ROWS = 8
MESH = pl.DeviceIdType.MESH
FACTOR = 1.0 / math.sqrt(HEAD_DIM)
BLOCKED = -30000.0
TWICE = math.log(2.0) / FACTOR
COMPUTE = True


def wait_bytes(ref, sem):
    pltpu.make_async_copy(ref, ref, sem).wait()


def rms_inverse(wide):
    return lax.rsqrt(jnp.mean(wide * wide, axis=-1, keepdims=True) + EPS)


def rms_back(wide, inverse, gain_row, upstream):
    scaled = upstream * gain_row
    inner = jnp.mean(wide * scaled, axis=-1, keepdims=True)
    grad = inverse * scaled - wide * (inverse * inverse * inverse * inner)
    return grad.astype(jnp.bfloat16), jnp.sum(upstream * wide * inverse, axis=0, keepdims=True)


def kernel(
    sizes,
    q_in, k_in, v_in, c_in, g_in, info,
    dq_out, dk_out, dv_out, gain_out,
    xq, xk, xv, cot, oq, ok, ov,
    qa, ka, kt, live, wbuf, gbuf, dk_acc, dv_acc,
    gx, gy, ysrc, gains, gacc, hz, hx, hy, hsrc, hsrc2,
    fsend, frecv, csend, crecv, rsend, orecv, gsend, grecv,
):
    chips, shard, per_chip = sizes
    seq = lax.axis_index("seq")
    dp = lax.axis_index("dp")
    chip, core = seq // 2, seq % 2
    row, col = dp // COLS, dp % COLS
    total = 2 * chips * shard
    blocks = total // BLOCK

    barrier = pltpu.get_barrier_semaphore()

    def greet_seq(i, carry):
        pl.semaphore_signal(barrier, inc=1, device_id={"seq": (seq + i) % (2 * chips)}, device_id_type=MESH)
        return carry

    def greet_col(i, carry):
        pl.semaphore_signal(barrier, inc=1, device_id={"dp": row * COLS + (col + i) % COLS}, device_id_type=MESH)
        return carry

    def greet_row(i, carry):
        pl.semaphore_signal(barrier, inc=1, device_id={"dp": (row + i) % ROWS * COLS + col}, device_id_type=MESH)
        return carry

    lax.fori_loop(1, 2 * chips, greet_seq, 0)
    lax.fori_loop(1, COLS, greet_col, 0)
    lax.fori_loop(1, ROWS, greet_row, 0)
    pl.semaphore_wait(barrier, 2 * chips - 1 + COLS - 1 + ROWS - 1)

    arrays = ((q_in, xq), (k_in, xk), (v_in, xv))
    my_rows = pl.ds(pl.multiple_of(seq * shard, shard), shard)

    def send_gx(i, carry):
        pltpu.make_async_remote_copy(
            src_ref=g_in, dst_ref=gx.at[col], send_sem=gsend.at[0], recv_sem=grecv.at[0],
            device_id={"dp": row * COLS + (col + i) % COLS}, device_id_type=MESH,
        ).start()
        return carry

    lax.fori_loop(1, COLS, send_gx, 0)
    gx[col] = g_in[...]

    def far(i):
        half = (i + 1) // 2
        return (chip + chips // 2 + half * (1 - 2 * (i % 2))) % chips

    def send_cot(i, carry):
        pltpu.make_async_remote_copy(
            src_ref=c_in.at[0], dst_ref=cot.at[chip, core], send_sem=csend.at[0], recv_sem=crecv.at[0],
            device_id={"seq": 2 * far(i) + core}, device_id_type=MESH,
        ).start()
        return carry

    lax.fori_loop(0, chips - 1, send_cot, 0)
    pltpu.make_async_copy(c_in.at[0], cot.at[chip, core], crecv.at[0]).start()

    def spread_head(which):
        owner, slot = which % 2, which // 2

        def to_chip(target, start_kind):
            lanes = pl.ds(pl.multiple_of((target * per_chip + which) * HEAD_DIM, HEAD_DIM), HEAD_DIM)
            for index, (source, landing) in enumerate(arrays):
                src = source.at[0, :, lanes]
                dst = landing.at[slot, my_rows, :]
                if start_kind == "local":
                    pltpu.make_async_copy(src, dst, frecv.at[slot, index]).start()
                else:
                    pltpu.make_async_remote_copy(
                        src_ref=src, dst_ref=dst, send_sem=fsend.at[index], recv_sem=frecv.at[slot, index],
                        device_id={"seq": 2 * target + owner}, device_id_type=MESH,
                    ).start()

        def remote(i, carry):
            to_chip(far(i), "remote")
            return carry

        lax.fori_loop(0, chips - 1, remote, 0)

        @pl.when(core == owner)
        def _():
            to_chip(chip, "local")

        @pl.when(core != owner)
        def _():
            to_chip(chip, "remote")

    for which in range(per_chip):
        spread_head(which)

    wait_bytes(gx.at[pl.ds(0, COLS - 1)], grecv.at[0])
    ysrc[...] = gx[0] + gx[1] + gx[2] + gx[3]

    lanes = lax.broadcasted_iota(jnp.int32, (TILE, HEAD_DIM), 1)
    rows64 = lax.broadcasted_iota(jnp.int32, (TILE, HEAD_DIM), 0)
    length = info[4:5, :]
    high = float(ml_dtypes.bfloat16(TWICE))
    low = float(ml_dtypes.bfloat16(TWICE - high))

    def mask_tile(j, carry):
        count = jnp.zeros((1, HEAD_DIM), jnp.int32)
        for n in range(4):
            count = count + (info[n : n + 1, :] == j).astype(jnp.int32)
        count = jnp.broadcast_to(count, (TILE, HEAD_DIM))
        usable = jnp.logical_and(count > 0, j * TILE + rows64 < length)
        first = jnp.where(usable, jnp.where(count > 1, high, 0.0), BLOCKED)
        second = jnp.where(count > 1, low, 0.0)
        bias = jnp.where(lanes < 32, first, jnp.where(lanes < 64, second, 0.0))
        here = pl.ds(pl.multiple_of(j * TILE, TILE), TILE)
        ka[here, HEAD_DIM:] = bias.astype(jnp.bfloat16)
        mark = jnp.logical_and(lanes % 32 == j, lanes < 64)
        qa[here, HEAD_DIM:] = jnp.where(mark, 1.0, 0.0).astype(jnp.bfloat16)
        return carry

    lax.fori_loop(0, total // TILE, mask_tile, 0)
    gacc[...] = jnp.zeros_like(gacc)

    def send_gy(i, carry):
        pltpu.make_async_remote_copy(
            src_ref=ysrc, dst_ref=gy.at[row], send_sem=gsend.at[1], recv_sem=grecv.at[1],
            device_id={"dp": (row + i) % ROWS * COLS + col}, device_id_type=MESH,
        ).start()
        return carry

    lax.fori_loop(1, ROWS, send_gy, 0)
    gy[row] = ysrc[...]

    wait_bytes(cot.at[:, 0], crecv.at[0])
    partner = 2 * chip + 1 - core
    forward = pltpu.make_async_remote_copy(
        src_ref=cot.at[:, core], dst_ref=cot.at[:, core], send_sem=csend.at[1], recv_sem=crecv.at[1],
        device_id={"seq": partner}, device_id_type=MESH,
    )
    forward.start()
    wait_bytes(gy.at[pl.ds(0, ROWS - 1)], grecv.at[1])
    summed = gy[0]
    for i in range(1, ROWS):
        summed = summed + gy[i]
    gains[...] = summed
    forward.wait()

    def live_block(i, carry):
        tokens = i * BLOCK + lax.broadcasted_iota(jnp.int32, (BLOCK, HEAD_DIM), 0)
        block = cot[i].reshape(BLOCK, HEAD_DIM).astype(jnp.float32)
        here = pl.ds(pl.multiple_of(i * BLOCK, BLOCK), BLOCK)
        live[here, :] = jnp.where(tokens < length, block, 0.0).astype(jnp.bfloat16)
        return carry

    lax.fori_loop(0, blocks, live_block, 0)
    gain_q, gain_k = gains[0:1, :], gains[1:2, :]

    def one_head(slot, carry):
        for index, (_, landing) in enumerate(arrays):
            wait_bytes(landing.at[slot], frecv.at[slot, index])

        def block_rows(i):
            return pl.ds(pl.multiple_of(i * BLOCK, BLOCK), BLOCK)

        def prepare(i, carry):
            here = block_rows(i)
            wide = xk[slot, here, :].astype(jnp.float32)
            norm = (wide * rms_inverse(wide) * gain_k).astype(jnp.bfloat16)
            ka[here, :HEAD_DIM] = norm
            kt[:, here] = norm.T
            wide = xq[slot, here, :].astype(jnp.float32)
            qa[here, :HEAD_DIM] = (wide * rms_inverse(wide) * gain_q).astype(jnp.bfloat16)
            zero = jnp.zeros((BLOCK, HEAD_DIM), jnp.float32)
            dk_acc[here, :] = zero
            dv_acc[here, :] = zero
            return carry

        lax.fori_loop(0, blocks, prepare, 0)

        nt = (((1,), (1,)), ((), ()))

        def query_block(b, carry):
            here = block_rows(b)
            q_block = qa[here, :]
            q_norm = q_block[:, :HEAD_DIM]
            live_rows = live[here, :]

            def scores(i, sums):
                den, mixed = sums
                keys = block_rows(i)
                logits = lax.dot_general(ka[keys, :], q_block, nt, preferred_element_type=jnp.float32)
                weight = jnp.exp(logits * FACTOR)
                grad = lax.dot_general(xv[slot, keys, :], live_rows, nt, preferred_element_type=jnp.float32)
                wbuf[keys, :] = weight
                gbuf[keys, :] = grad
                den = den + jnp.sum(weight, axis=0, keepdims=True)
                mixed = mixed + jnp.sum(weight * grad, axis=0, keepdims=True)
                return den, mixed

            zero = jnp.zeros((1, BLOCK), jnp.float32)
            den, mixed = lax.fori_loop(0, blocks, scores, (zero, zero))
            inv = 1.0 / den
            diag = mixed * inv

            def grads(i, dq_t):
                keys = block_rows(i)
                prob = wbuf[keys, :] * inv
                prob_low = prob.astype(jnp.bfloat16)
                grad_score = (prob * (gbuf[keys, :] - diag)).astype(jnp.bfloat16)
                dv_acc[keys, :] += jnp.dot(prob_low, live_rows, preferred_element_type=jnp.float32)
                dk_acc[keys, :] += jnp.dot(grad_score, q_norm, preferred_element_type=jnp.float32)
                return dq_t + jnp.dot(kt[:, keys], grad_score, preferred_element_type=jnp.float32)

            dq_t = lax.fori_loop(0, blocks, grads, jnp.zeros((HEAD_DIM, BLOCK), jnp.float32))
            upstream = (dq_t.T * FACTOR).astype(jnp.bfloat16).astype(jnp.float32)
            wide = xq[slot, here, :].astype(jnp.float32)
            grad, gain = rms_back(wide, rms_inverse(wide), gain_q, upstream)
            oq[slot, here, :] = grad
            gacc[0:1, :] += gain
            return carry

        if COMPUTE:
            lax.fori_loop(0, blocks, query_block, 0)

        def finish(i, carry):
            here = block_rows(i)
            upstream = (dk_acc[here, :] * FACTOR).astype(jnp.bfloat16).astype(jnp.float32)
            wide = xk[slot, here, :].astype(jnp.float32)
            grad, gain = rms_back(wide, rms_inverse(wide), gain_k, upstream)
            ok[slot, here, :] = grad
            ov[slot, here, :] = dv_acc[here, :].astype(jnp.bfloat16)
            gacc[1:2, :] += gain
            return carry

        lax.fori_loop(0, blocks, finish, 0)

        head = chip * per_chip + core + 2 * slot
        out_lanes = pl.ds(pl.multiple_of(head * HEAD_DIM, HEAD_DIM), HEAD_DIM)
        results = ((oq, dq_out), (ok, dk_out), (ov, dv_out))

        def give_back(target, core_to, local):
            other = 2 * target + core_to
            rows = pl.ds(pl.multiple_of(other * shard, shard), shard)
            for index, (source, landing) in enumerate(results):
                src = source.at[slot, rows, :]
                dst = landing.at[0, :, out_lanes]
                if local:
                    pltpu.make_async_copy(src, dst, orecv.at[index]).start()
                else:
                    pltpu.make_async_remote_copy(
                        src_ref=src, dst_ref=dst, send_sem=rsend.at[slot, index], recv_sem=orecv.at[index],
                        device_id={"seq": other}, device_id_type=MESH,
                    ).start()

        def back(i, carry):
            give_back(far(i), core, False)
            give_back(far(i), 1 - core, False)
            return carry

        lax.fori_loop(0, chips - 1, back, 0)
        give_back(chip, 1 - core, False)
        give_back(chip, core, True)
        return carry

    lax.fori_loop(0, 2 - core, one_head, 0)

    hsrc[...] = gacc[...]

    def send_hz(i, carry):
        pltpu.make_async_remote_copy(
            src_ref=hsrc, dst_ref=hz.at[seq], send_sem=gsend.at[2], recv_sem=grecv.at[2],
            device_id={"seq": (seq + i) % (2 * chips)}, device_id_type=MESH,
        ).start()
        return carry

    lax.fori_loop(1, 2 * chips, send_hz, 0)
    hz[seq] = hsrc[...]
    wait_bytes(hz.at[pl.ds(0, 2 * chips - 1)], grecv.at[2])
    summed = hz[0]
    for i in range(1, 2 * chips):
        summed = summed + hz[i]
    hsrc2[0] = summed

    def send_hx(i, carry):
        pltpu.make_async_remote_copy(
            src_ref=hsrc2.at[0], dst_ref=hx.at[col], send_sem=gsend.at[3], recv_sem=grecv.at[3],
            device_id={"dp": row * COLS + (col + i) % COLS}, device_id_type=MESH,
        ).start()
        return carry

    lax.fori_loop(1, COLS, send_hx, 0)
    hx[col] = summed
    wait_bytes(hx.at[pl.ds(0, COLS - 1)], grecv.at[3])
    summed = hx[0] + hx[1] + hx[2] + hx[3]
    hsrc2[1] = summed

    def send_hy(i, carry):
        pltpu.make_async_remote_copy(
            src_ref=hsrc2.at[1], dst_ref=hy.at[row], send_sem=gsend.at[4], recv_sem=grecv.at[4],
            device_id={"dp": (row + i) % ROWS * COLS + col}, device_id_type=MESH,
        ).start()
        return carry

    lax.fori_loop(1, ROWS, send_hy, 0)
    hy[row] = summed
    wait_bytes(hy.at[pl.ds(0, ROWS - 1)], grecv.at[4])
    summed = hy[0]
    for i in range(1, ROWS):
        summed = summed + hy[i]
    gain_out[...] = summed

    wait_bytes(gx.at[pl.ds(0, COLS - 1)], gsend.at[0])
    wait_bytes(gy.at[pl.ds(0, ROWS - 1)], gsend.at[1])
    wait_bytes(hz.at[pl.ds(0, 2 * chips - 1)], gsend.at[2])
    wait_bytes(hx.at[pl.ds(0, COLS - 1)], gsend.at[3])
    wait_bytes(hy.at[pl.ds(0, ROWS - 1)], gsend.at[4])
    wait_bytes(cot.at[pl.ds(0, chips - 1), 0], csend.at[0])
    count = chips * per_chip
    for index, (source, _) in enumerate(arrays):
        @pl.when(core == 0)
        def _():
            wait_bytes(source.at[0, :, pl.ds(0, (count - 2) * HEAD_DIM)], fsend.at[index])

        @pl.when(core == 1)
        def _():
            wait_bytes(source.at[0, :, pl.ds(0, (count - 1) * HEAD_DIM)], fsend.at[index])

    def sent(slot, carry):
        for index, buffer in enumerate((oq, ok, ov)):
            wait_bytes(buffer.at[slot, pl.ds(0, total - shard), :], rsend.at[slot, index])
        return carry

    lax.fori_loop(0, 2 - core, sent, 0)
    for index, out in enumerate((dq_out, dk_out, dv_out)):
        wait_bytes(out, orecv.at[index])


def body(queries, key_states, value_states, cotangent, norm_gains, tile_lists, clip_lengths):
    seq_count = lax.axis_size("seq")
    dp_count = lax.axis_size("dp")
    dp = lax.axis_index("dp")
    shard, width = queries.shape[1], queries.shape[2]
    heads = width // HEAD_DIM
    chips = seq_count // 2
    per_chip = heads // chips
    total = shard * seq_count
    owned = norm_gains.shape[1]
    lane = jnp.arange(HEAD_DIM, dtype=jnp.int32)
    spread = jnp.where(lane // owned == dp, jnp.tile(norm_gains, (1, dp_count)), 0.0)
    g_in = jnp.concatenate([spread, jnp.zeros((6, HEAD_DIM), jnp.float32)], 0)
    lists = jnp.tile(tile_lists.T, (1, HEAD_DIM // tile_lists.shape[0]))
    info = jnp.concatenate([lists, jnp.broadcast_to(clip_lengths[:, None], (4, HEAD_DIM))], 0)
    bf, f32 = jnp.bfloat16, jnp.float32
    hbm = pl.BlockSpec(memory_space=pl.ANY)
    vmem = pl.BlockSpec(memory_space=pltpu.VMEM)
    dma = pltpu.SemaphoreType.DMA
    shaped = jax.ShapeDtypeStruct(queries.shape, bf)
    pair = pltpu.VMEM((2, total, HEAD_DIM), bf)
    tiny = lambda n: pltpu.VMEM((n, 8, HEAD_DIM), f32)
    dq, dk, dv, gain_sum = pl.pallas_call(
        functools.partial(kernel, (chips, shard, per_chip)),
        out_shape=(shaped, shaped, shaped, jax.ShapeDtypeStruct((8, HEAD_DIM), f32)),
        in_specs=[hbm, hbm, hbm, hbm, vmem, vmem],
        out_specs=(hbm, hbm, hbm, vmem),
        scratch_shapes=[
            pair, pair, pair, pltpu.VMEM((chips, 2, shard, HEAD_DIM), bf), pair, pair, pair,
            pltpu.VMEM((total, 2 * HEAD_DIM), bf), pltpu.VMEM((total, 2 * HEAD_DIM), bf),
            pltpu.VMEM((HEAD_DIM, total), bf), pltpu.VMEM((total, HEAD_DIM), bf),
            pltpu.VMEM((total, BLOCK), f32), pltpu.VMEM((total, BLOCK), f32),
            pltpu.VMEM((total, HEAD_DIM), f32), pltpu.VMEM((total, HEAD_DIM), f32),
            tiny(COLS), tiny(ROWS), pltpu.VMEM((8, HEAD_DIM), f32), pltpu.VMEM((8, HEAD_DIM), f32),
            pltpu.VMEM((8, HEAD_DIM), f32), tiny(seq_count), tiny(COLS), tiny(ROWS),
            pltpu.VMEM((8, HEAD_DIM), f32), tiny(2),
            dma((3,)), dma((2, 3)), dma((2,)), dma((2,)), dma((2, 3)), dma((3,)), dma((5,)), dma((5,)),
        ],
        compiler_params=pltpu.CompilerParams(
            collective_id=0, has_side_effects=True, vmem_limit_bytes=48 * 1024 * 1024
        ),
    )(queries, key_states, value_states, cotangent, g_in, info)
    norm_factor = 1.0 / math.sqrt(dp_count * total * heads)
    gain_grad = lax.dynamic_slice_in_dim(gain_sum[:2], dp * owned, owned, 1) * norm_factor
    return dq, dk, dv, gain_grad


def solution(mesh):
    placed = (
        P("dp", "seq", None),
        P("dp", "seq", None),
        P("dp", "seq", None),
        P("dp", "seq", None),
        P(None, "dp"),
        P(),
        P("dp"),
    )
    return jax.shard_map(
        body,
        mesh=mesh,
        in_specs=placed,
        out_specs=(P("dp", "seq", None), P("dp", "seq", None), P("dp", "seq", None), P(None, "dp")),
        check_vma=False,
    )
```

time: 484 us -> 157 us (0.32)
  waiting for transfers between devices: 149 us -> 0 us
  Pallas kernels: 0 us -> 148 us
  blocking collectives: 128 us -> 0 us
  local copies, waits for them, and re-layouts: 87.9 us -> 7.56 us
  other arithmetic: 52.3 us -> 0.65 us
  starting transfers between devices: 43 us -> 0 us
  matrix products: 18.2 us -> 0 us
    all_to_all x6 -> x0, waiting for transfers between devices: 149 us -> none  [the longest x1 50 us: body(): lax.all_to_all(stacked.reshape(2, seq_count, token_count, feature), 'seq'...]
    pallas_call x0 -> x1, Pallas kernels: none -> 148 us  [body(): pl.pallas_call(functools.partial(kernel, (chips, shard, per_chip)), out_s...]
    unnamed x1 -> x0, blocking collectives: 58.3 us -> none
    all_to_all x6 -> x0, starting transfers between devices: 43 us -> none  [the longest x1 19.1 us: body(): lax.all_to_all(send_query, 'seq', split_axis=0, concat_axis=0, tiled=True)]
    psum x1 -> x0, blocking collectives: 37.8 us -> none  [body(): over_seq = lax.psum(gain_terms, 'seq')]
    all_gather x1 -> x0, blocking collectives: 32.2 us -> none  [body(): gain_rows = lax.all_gather(norm_gains, 'dp', axis=1, tiled=True)]
    scatter-add x4 -> x0, other arithmetic: 29 us -> none  [the longest x2 14.9 us: tile_step(): acc_values.at[where_rows]]
    convert_element_type x7 -> x0, local copies, waits for them, and re-layouts: 20.3 us -> none  [the longest x3 14.8 us: body(): stacked = stacked.reshape(2, tile_count, TILE, feature).astype(jnp.bfloat16)]
  transfers between devices with their start and end apart: 6 -> 0, of which waited for: 5 -> 0; matrix products, arithmetic and copies ran while one was open for 10% -> 0% of each run, Pallas kernels for 0% -> 0%
where the time goes in v1:
time: 157 us
  Pallas kernels  148 us (94%)
  local copies, waits for them, and re-layouts  7.56 us (5%)
    pallas_call x1, Pallas kernels, body(): pl.pallas_call(functools.partial(kernel, (chips, shard, per_chip)), out_s...  148 us
    unnamed x15, local copies, waits for them, and re-layouts  7.36 us

profile of v1, /device:TPU:1, one launch (start us, length us, event | category | flops | bytes accessed | tf_op | source)
XLA Modules:
  0.0 157.1 jit_solution(1671993698999344495)
XLA Ops:
  0.6 0.0 copy-start.5
  0.7 0.7 copy-done.5
  1.3 0.0 copy-start.3
  1.3 0.1 tile.9
  1.4 0.0 copy-start.4
  1.5 0.7 copy-done.4
  2.1 0.1 tile.21
  2.9 0.0 copy-done.3
  2.9 0.0 copy-start
  2.9 1.1 copy-done
  4.0 0.0 copy-start.1
  4.0 1.1 copy-done.1
  5.2 0.0 copy-start.2
  5.2 1.1 copy-done.2
  6.3 147.5 %shard_map.102 = (bf16[1,128,3072]{2,1,0:T(8,128)(2,1)S(1)}, bf16[1,128,3072]{2,1,0:T(8,128)(2,1)S(1)}, bf16[1,128,3072]{2,1,0:T(8,128)(2,1)S(1)}, f32[8,128]{1,0:T(8,128)S(1)}) custom-call(bf16[1,128,3072]{2,1,0:T(8,128)(2,1)S(1)} %copy-done, bf16[1,128,3072]{2,1,0:T(8,128)(2,1)S(1)} %copy-done.1, bf16[1,128,3072]{2,1,0:T(8,128)(2,1)S(1)} %copy-done.2, ...), custom_call_target="tpu_custom_call" | custom-call | tf_op jit(solution)/shard_map/pallas_call | solution.py:400
  153.8 0.6 dynamic-slice_multiply_fusion
  154.5 0.9 copy.15
  155.3 0.9 copy.16
  156.2 0.9 copy.17
  (7 shorter events, 0.0 us)
Async XLA Ops:
  0.6 0.7 copy-start.5
  1.3 1.6 copy-start.3
  1.4 0.7 copy-start.4
  2.9 1.1 copy-start
  4.0 1.1 copy-start.1
  5.2 1.1 copy-start.2

commit v2 on v1

v2 whole, which is shorter than its diff:
```python
import functools
import math


import jax
import jax.numpy as jnp
from jax import lax
from jax.experimental import pallas as pl
from jax.experimental.pallas import tpu as pltpu
import ml_dtypes
from jax.sharding import PartitionSpec as P

HEAD_DIM = 128
TILE = 64
PIECES = 4
EPS = 1e-06
BLOCK = 256
MESH = pl.DeviceIdType.MESH
FACTOR = 1.0 / math.sqrt(HEAD_DIM)
BLOCKED = -30000.0
TWICE = math.log(2.0) / FACTOR


def wait_bytes(ref, sem):
    pltpu.make_async_copy(ref, ref, sem).wait()


def wait_many(ref, count, sem):
    if count:
        wait_bytes(ref.at[pl.ds(0, count)], sem)


def total_of(ref):
    total = ref[0]
    for i in range(1, ref.shape[0]):
        total = total + ref[i]
    return total


def rms_inverse(wide):
    return lax.rsqrt(jnp.mean(wide * wide, axis=-1, keepdims=True) + EPS)


def rms_back(wide, inverse, gain_row, upstream):
    scaled = upstream * gain_row
    inner = jnp.mean(wide * scaled, axis=-1, keepdims=True)
    grad = inverse * scaled - wide * (inverse * inverse * inverse * inner)
    return grad.astype(jnp.bfloat16), jnp.sum(upstream * wide * inverse, axis=0, keepdims=True)


def kernel(
    sizes,
    q_in, k_in, v_in, c_in, g_hbm, lists_hbm, lengths,
    dq_out, dk_out, dv_out, gain_out,
    xq, xk, xv, cot, oq, ok, ov,
    qa, ka, kt, live, wbuf, gbuf, dk_acc, dv_acc,
    gsrc, gx, gy, ysrc, gains, gacc, hz, hx, hy, hsrc, hsrc2,
    g_raw, lists, tsem,
    fsend, frecv, csend, crecv, osem, psem, rsend, orecv, gsend, grecv,
):
    chips, shard, per_chip, cols, rows = sizes
    seq = lax.axis_index("seq")
    dp = lax.axis_index("dp")
    chip, core = seq // 2, seq % 2
    row, col = dp // cols, dp % cols
    total = 2 * chips * shard
    blocks = total // BLOCK

    small = ((g_hbm, g_raw), (lists_hbm, lists))
    for index, (source, landing) in enumerate(small):
        pltpu.make_async_copy(source, landing, tsem.at[index]).start()

    barrier = pltpu.get_barrier_semaphore()

    def greet_seq(i, carry):
        pl.semaphore_signal(barrier, inc=1, device_id={"seq": (seq + i) % (2 * chips)}, device_id_type=MESH)
        return carry

    def greet_col(i, carry):
        pl.semaphore_signal(barrier, inc=1, device_id={"dp": row * cols + (col + i) % cols}, device_id_type=MESH)
        return carry

    def greet_row(i, carry):
        pl.semaphore_signal(barrier, inc=1, device_id={"dp": (row + i) % rows * cols + col}, device_id_type=MESH)
        return carry

    lax.fori_loop(1, 2 * chips, greet_seq, 0)
    lax.fori_loop(1, cols, greet_col, 0)
    lax.fori_loop(1, rows, greet_row, 0)
    pl.semaphore_wait(barrier, 2 * chips - 1 + cols - 1 + rows - 1)

    arrays = ((q_in, xq), (k_in, xk), (v_in, xv))
    my_rows = pl.ds(pl.multiple_of(seq * shard, shard), shard)

    def near(i):
        half = i // 2 + 1
        return (chip + half * (1 - 2 * (i % 2)) + chips) % chips

    def pass_on(origin, step, way, side):
        source = c_in.at[0] if step == 1 else cot.at[origin, core]
        pltpu.make_async_remote_copy(
            src_ref=source, dst_ref=cot.at[origin, core],
            send_sem=csend.at[side, step - 1], recv_sem=crecv.at[side, step - 1],
            device_id={"seq": 2 * ((chip + way + chips) % chips) + core}, device_id_type=MESH,
        ).start()

    def passed(step, side, sems):
        wait_bytes(cot.at[0, 0], sems.at[side, step - 1])

    own_cot = pltpu.make_async_copy(c_in.at[0], cot.at[chip, core], osem)
    own_cot.start()
    last_step = chips // 2

    def spread_head(which):
        owner, slot = which % 2, which // 2

        def to_chip(target, start_kind):
            lanes = pl.ds(pl.multiple_of((target * per_chip + which) * HEAD_DIM, HEAD_DIM), HEAD_DIM)
            for index, (source, landing) in enumerate(arrays):
                src = source.at[0, :, lanes]
                dst = landing.at[slot, my_rows, :]
                if start_kind == "local":
                    pltpu.make_async_copy(src, dst, frecv.at[slot, index]).start()
                else:
                    pltpu.make_async_remote_copy(
                        src_ref=src, dst_ref=dst, send_sem=fsend.at[index], recv_sem=frecv.at[slot, index],
                        device_id={"seq": 2 * target + owner}, device_id_type=MESH,
                    ).start()

        def remote(i, carry):
            to_chip(near(i), "remote")
            return carry

        def at_home():
            @pl.when(core == owner)
            def _():
                to_chip(chip, "local")

            @pl.when(core != owner)
            def _():
                to_chip(chip, "remote")

        return remote, at_home

    remote, at_home = spread_head(0)
    for step in range(1, last_step):
        for side, way in ((0, 1), (1, -1)):
            if step > 1:
                passed(step - 1, side, crecv)
            pass_on((chip - (step - 1) * way + chips) % chips, step, way, side)
        remote(2 * step - 2, 0)
        remote(2 * step - 1, 0)
    for side in range(2):
        passed(last_step - 1, side, crecv)
    way = 1 - 2 * core
    pass_on((chip - (last_step - 1) * way + chips) % chips, last_step, way, 0)
    remote(chips - 2, 0)
    at_home()
    for which in range(1, per_chip):
        remote, at_home = spread_head(which)
        lax.fori_loop(0, chips - 1, remote, 0)
        at_home()

    for index, (source, landing) in enumerate(small):
        pltpu.make_async_copy(source, landing, tsem.at[index]).wait()

    lane = lax.broadcasted_iota(jnp.int32, (8, HEAD_DIM), 1)
    sub = lax.broadcasted_iota(jnp.int32, (8, HEAD_DIM), 0)
    owned = g_raw.shape[1]
    spread = jnp.zeros((8, HEAD_DIM), jnp.float32)
    for r in range(2):
        for c in range(owned):
            spot = jnp.logical_and(sub == r, lane == dp * owned + c)
            spread = jnp.where(spot, g_raw[r, c], spread)
    gsrc[...] = spread

    lanes = lax.broadcasted_iota(jnp.int32, (TILE, HEAD_DIM), 1)
    places = lax.broadcasted_iota(jnp.int32, (TILE, HEAD_DIM), 0)
    length = lengths[0]
    high = float(ml_dtypes.bfloat16(TWICE))
    low = float(ml_dtypes.bfloat16(TWICE - high))

    def mask_tile(t, carry):
        named = jnp.zeros((TILE, HEAD_DIM), jnp.int32)
        for n in range(lists.shape[0]):
            named = named + (lanes % 32 == lists[n, t]).astype(jnp.int32)
        first = jnp.where(named > 0, jnp.where(named > 1, high, 0.0), BLOCKED)
        second = jnp.where(named > 1, low, 0.0)
        bias = jnp.where(lanes < 32, first, jnp.where(lanes < 64, second, 0.0))
        bias = jnp.where(lanes == 64, BLOCKED, bias)
        here = pl.ds(pl.multiple_of(t * TILE, TILE), TILE)
        qa[here, HEAD_DIM:] = bias.astype(jnp.bfloat16)
        mark = jnp.logical_and(lanes % 32 == t, lanes < 64)
        past = jnp.logical_and(lanes == 64, t * TILE + places >= length)
        ka[here, HEAD_DIM:] = jnp.where(jnp.logical_or(mark, past), 1.0, 0.0).astype(jnp.bfloat16)
        return carry

    lax.fori_loop(0, total // TILE, mask_tile, 0)
    def send_gx(i, carry):
        pltpu.make_async_remote_copy(
            src_ref=gsrc, dst_ref=gx.at[col], send_sem=gsend.at[0], recv_sem=grecv.at[0],
            device_id={"dp": row * cols + (col + i) % cols}, device_id_type=MESH,
        ).start()
        return carry

    lax.fori_loop(1, cols, send_gx, 0)
    gx[col] = gsrc[...]

    gacc[...] = jnp.zeros_like(gacc)
    wait_many(gx, cols - 1, grecv.at[0])
    ysrc[...] = total_of(gx)

    passed(last_step, 0, crecv)
    own_cot.wait()
    partner = 2 * chip + 1 - core
    forward = pltpu.make_async_remote_copy(
        src_ref=cot.at[:, core], dst_ref=cot.at[:, core], send_sem=psem.at[0], recv_sem=psem.at[1],
        device_id={"seq": partner}, device_id_type=MESH,
    )
    forward.start()
    def send_gy(i, carry):
        pltpu.make_async_remote_copy(
            src_ref=ysrc, dst_ref=gy.at[row], send_sem=gsend.at[1], recv_sem=grecv.at[1],
            device_id={"dp": (row + i) % rows * cols + col}, device_id_type=MESH,
        ).start()
        return carry

    lax.fori_loop(1, rows, send_gy, 0)
    gy[row] = ysrc[...]

    wait_many(gy, rows - 1, grecv.at[1])
    gains[...] = total_of(gy)
    forward.wait()

    def live_block(i, carry):
        tokens = i * BLOCK + lax.broadcasted_iota(jnp.int32, (BLOCK, HEAD_DIM), 0)
        block = cot[i].reshape(BLOCK, HEAD_DIM).astype(jnp.float32)
        here = pl.ds(pl.multiple_of(i * BLOCK, BLOCK), BLOCK)
        live[here, :] = jnp.where(tokens < length, block, 0.0).astype(jnp.bfloat16)
        return carry

    lax.fori_loop(0, blocks, live_block, 0)
    gain_q, gain_k = gains[0:1, :], gains[1:2, :]

    def one_head(slot, carry):
        for index, (_, landing) in enumerate(arrays):
            wait_bytes(landing.at[slot], frecv.at[slot, index])

        def block_rows(i):
            return pl.ds(pl.multiple_of(i * BLOCK, BLOCK), BLOCK)

        def prepare(i, carry):
            here = block_rows(i)
            wide = xk[slot, here, :].astype(jnp.float32)
            norm = (wide * rms_inverse(wide) * gain_k).astype(jnp.bfloat16)
            ka[here, :HEAD_DIM] = norm
            kt[:, here] = norm.T
            wide = xq[slot, here, :].astype(jnp.float32)
            qa[here, :HEAD_DIM] = (wide * rms_inverse(wide) * gain_q).astype(jnp.bfloat16)
            zero = jnp.zeros((BLOCK, HEAD_DIM), jnp.float32)
            dk_acc[here, :] = zero
            dv_acc[here, :] = zero
            return carry

        lax.fori_loop(0, blocks, prepare, 0, unroll=2)

        nt = (((1,), (1,)), ((), ()))

        def query_block(b, carry):
            here = block_rows(b)
            q_block = qa[here, :]
            q_norm = q_block[:, :HEAD_DIM]
            live_rows = live[here, :]

            def scores(i, sums):
                den, mixed = sums
                keys = block_rows(i)
                logits = lax.dot_general(ka[keys, :], q_block, nt, preferred_element_type=jnp.float32)
                weight = jnp.exp(logits * FACTOR)
                grad = lax.dot_general(xv[slot, keys, :], live_rows, nt, preferred_element_type=jnp.float32)
                wbuf[keys, :] = weight
                gbuf[keys, :] = grad
                den = den + jnp.sum(weight, axis=0, keepdims=True)
                mixed = mixed + jnp.sum(weight * grad, axis=0, keepdims=True)
                return den, mixed

            zero = jnp.zeros((1, BLOCK), jnp.float32)
            den, mixed = lax.fori_loop(0, blocks, scores, (zero, zero), unroll=True)
            inv = 1.0 / den
            diag = mixed * inv

            def grads(i, dq_t):
                keys = block_rows(i)
                prob = wbuf[keys, :] * inv
                prob_low = prob.astype(jnp.bfloat16)
                grad_score = (prob * (gbuf[keys, :] - diag)).astype(jnp.bfloat16)
                dv_acc[keys, :] += jnp.dot(prob_low, live_rows, preferred_element_type=jnp.float32)
                dk_acc[keys, :] += jnp.dot(grad_score, q_norm, preferred_element_type=jnp.float32)
                return dq_t + jnp.dot(kt[:, keys], grad_score, preferred_element_type=jnp.float32)

            dq_t = lax.fori_loop(
                0, blocks, grads, jnp.zeros((HEAD_DIM, BLOCK), jnp.float32), unroll=True
            )
            upstream = (dq_t.T * FACTOR).astype(jnp.bfloat16).astype(jnp.float32)
            wide = xq[slot, here, :].astype(jnp.float32)
            grad, gain = rms_back(wide, rms_inverse(wide), gain_q, upstream)
            oq[slot, here, :] = grad
            gacc[0:1, :] += gain
            return carry

        lax.fori_loop(0, blocks, query_block, 0)

        def finish(i, carry):
            here = block_rows(i)
            upstream = (dk_acc[here, :] * FACTOR).astype(jnp.bfloat16).astype(jnp.float32)
            wide = xk[slot, here, :].astype(jnp.float32)
            grad, gain = rms_back(wide, rms_inverse(wide), gain_k, upstream)
            ok[slot, here, :] = grad
            ov[slot, here, :] = dv_acc[here, :].astype(jnp.bfloat16)
            gacc[1:2, :] += gain
            return carry

        lax.fori_loop(0, blocks, finish, 0, unroll=2)

        @pl.when(slot == 1 - core)
        def _():
            hsrc[...] = gacc[...]
            hz[seq] = gacc[...]

        head = chip * per_chip + core + 2 * slot
        out_lanes = pl.ds(pl.multiple_of(head * HEAD_DIM, HEAD_DIM), HEAD_DIM)
        results = ((oq, dq_out), (ok, dk_out), (ov, dv_out))

        def give_back(target, core_to, local):
            other = 2 * target + core_to
            rows = pl.ds(pl.multiple_of(other * shard, shard), shard)
            for index, (source, landing) in enumerate(results):
                src = source.at[slot, rows, :]
                dst = landing.at[0, :, out_lanes]
                if local:
                    pltpu.make_async_copy(src, dst, orecv.at[index]).start()
                else:
                    pltpu.make_async_remote_copy(
                        src_ref=src, dst_ref=dst, send_sem=rsend.at[slot, index], recv_sem=orecv.at[index],
                        device_id={"seq": other}, device_id_type=MESH,
                    ).start()

        def back(i, carry):
            give_back(near(i), core, False)
            give_back(near(i), 1 - core, False)
            return carry

        lax.fori_loop(0, 2, back, 0)

        @pl.when(slot == 1 - core)
        def _():
            def send_hz(i, carry):
                pltpu.make_async_remote_copy(
                    src_ref=hsrc, dst_ref=hz.at[seq], send_sem=gsend.at[2], recv_sem=grecv.at[2],
                    device_id={"seq": (seq + i) % (2 * chips)}, device_id_type=MESH,
                ).start()
                return carry

            lax.fori_loop(1, 2 * chips, send_hz, 0)

        lax.fori_loop(2, chips - 1, back, 0)
        give_back(chip, 1 - core, False)
        give_back(chip, core, True)
        return carry

    lax.fori_loop(0, 2 - core, one_head, 0)

    wait_many(hz, 2 * chips - 1, grecv.at[2])
    summed = total_of(hz)
    hsrc2[0] = summed

    def send_hx(i, carry):
        pltpu.make_async_remote_copy(
            src_ref=hsrc2.at[0], dst_ref=hx.at[col], send_sem=gsend.at[3], recv_sem=grecv.at[3],
            device_id={"dp": row * cols + (col + i) % cols}, device_id_type=MESH,
        ).start()
        return carry

    lax.fori_loop(1, cols, send_hx, 0)
    hx[col] = summed
    wait_many(hx, cols - 1, grecv.at[3])
    summed = total_of(hx)
    hsrc2[1] = summed

    def send_hy(i, carry):
        pltpu.make_async_remote_copy(
            src_ref=hsrc2.at[1], dst_ref=hy.at[row], send_sem=gsend.at[4], recv_sem=grecv.at[4],
            device_id={"dp": (row + i) % rows * cols + col}, device_id_type=MESH,
        ).start()
        return carry

    lax.fori_loop(1, rows, send_hy, 0)
    hy[row] = summed
    wait_many(hy, rows - 1, grecv.at[4])
    gain_out[...] = total_of(hy)

    wait_many(gx, cols - 1, gsend.at[0])
    wait_many(gy, rows - 1, gsend.at[1])
    wait_many(hz, 2 * chips - 1, gsend.at[2])
    wait_many(hx, cols - 1, gsend.at[3])
    wait_many(hy, rows - 1, gsend.at[4])
    for step in range(1, last_step):
        passed(step, 0, csend)
        passed(step, 1, csend)
    passed(last_step, 0, csend)
    count = chips * per_chip
    for index, (source, _) in enumerate(arrays):
        @pl.when(core == 0)
        def _():
            wait_bytes(source.at[0, :, pl.ds(0, (count - 2) * HEAD_DIM)], fsend.at[index])

        @pl.when(core == 1)
        def _():
            wait_bytes(source.at[0, :, pl.ds(0, (count - 1) * HEAD_DIM)], fsend.at[index])

    def sent(slot, carry):
        for index, buffer in enumerate((oq, ok, ov)):
            wait_bytes(buffer.at[slot, pl.ds(0, total - shard), :], rsend.at[slot, index])
        return carry

    lax.fori_loop(0, 2 - core, sent, 0)
    for index, out in enumerate((dq_out, dk_out, dv_out)):
        wait_bytes(out, orecv.at[index])


def deliver(q_ref, k_ref, v_ref, gain_hbm, q_out, k_out, v_out, gain_out_hbm, held, gain_ref, gain_out, taken, given, gsem):
    shard = q_ref.shape[1]
    piece = shard // PIECES
    pairs = ((q_ref, q_out), (k_ref, k_out), (v_ref, v_out))

    def take(index, part):
        span = pl.ds(part * piece, piece)
        return pltpu.make_async_copy(pairs[index][0].at[0, span], held.at[index, span], taken.at[index, part])

    def give(index, part):
        span = pl.ds(part * piece, piece)
        return pltpu.make_async_copy(held.at[index, span], pairs[index][1].at[0, span], given.at[index, part])

    places = [(index, part) for index in range(3) for part in range(PIECES)]
    gain_take = pltpu.make_async_copy(gain_hbm, gain_ref, gsem.at[0])
    gain_give = pltpu.make_async_copy(gain_out, gain_out_hbm, gsem.at[1])
    gain_take.start()
    for place in places:
        take(*place).start()
    gain_take.wait()
    owned = gain_out.shape[1]
    turned = pltpu.roll(gain_ref[...], HEAD_DIM - lax.axis_index("dp") * owned, 1)
    count = lax.axis_size("dp") * lax.axis_size("seq") * shard * (q_ref.shape[2] // HEAD_DIM)
    gain_out[...] = turned[:2, :owned] * (1.0 / math.sqrt(count))
    for place in places:
        take(*place).wait()
        give(*place).start()
    gain_give.start()
    for place in places:
        give(*place).wait()
    gain_give.wait()


def body(queries, key_states, value_states, cotangent, norm_gains, tile_lists, clip_lengths):
    seq_count = lax.axis_size("seq")
    dp_count = lax.axis_size("dp")
    dp = lax.axis_index("dp")
    shard, width = queries.shape[1], queries.shape[2]
    heads = width // HEAD_DIM
    chips = seq_count // 2
    per_chip = heads // chips
    total = shard * seq_count
    owned = norm_gains.shape[1]
    cols = math.gcd(dp_count, 4)
    rows = dp_count // cols
    bf, f32 = jnp.bfloat16, jnp.float32
    hbm = pl.BlockSpec(memory_space=pltpu.HBM)
    vmem = pl.BlockSpec(memory_space=pltpu.VMEM)
    dma = pltpu.SemaphoreType.DMA
    shaped = jax.ShapeDtypeStruct(queries.shape, bf)
    pair = pltpu.VMEM((2, total, HEAD_DIM), bf)
    tiny = lambda n: pltpu.VMEM((n, 8, HEAD_DIM), f32)
    dq, dk, dv, gain_sum = pl.pallas_call(
        functools.partial(kernel, (chips, shard, per_chip, cols, rows)),
        out_shape=(shaped, shaped, shaped, jax.ShapeDtypeStruct((8, HEAD_DIM), f32)),
        in_specs=[hbm] * 6 + [pl.BlockSpec(memory_space=pltpu.SMEM)],
        out_specs=(hbm, hbm, hbm, vmem),
        scratch_shapes=[
            pair, pair, pair, pltpu.VMEM((chips, 2, shard, HEAD_DIM), bf), pair, pair, pair,
            pltpu.VMEM((total, 2 * HEAD_DIM), bf), pltpu.VMEM((total, 2 * HEAD_DIM), bf),
            pltpu.VMEM((HEAD_DIM, total), bf), pltpu.VMEM((total, HEAD_DIM), bf),
            pltpu.VMEM((total, BLOCK), f32), pltpu.VMEM((total, BLOCK), f32),
            pltpu.VMEM((total, HEAD_DIM), f32), pltpu.VMEM((total, HEAD_DIM), f32),
            pltpu.VMEM((8, HEAD_DIM), f32), tiny(cols), tiny(rows), pltpu.VMEM((8, HEAD_DIM), f32),
            pltpu.VMEM((8, HEAD_DIM), f32),
            pltpu.VMEM((8, HEAD_DIM), f32), tiny(seq_count), tiny(cols), tiny(rows),
            pltpu.VMEM((8, HEAD_DIM), f32), tiny(2),
            pltpu.SMEM(norm_gains.shape, f32), pltpu.SMEM(tile_lists.T.shape, jnp.int32),
            dma((2,)),
            dma((3,)), dma((2, 3)), dma((2, chips // 2)), dma((2, chips // 2)), dma(()), dma((2,)), dma((2, 3)), dma((3,)), dma((5,)), dma((5,)),
        ],
        compiler_params=pltpu.CompilerParams(
            collective_id=0, has_side_effects=True, vmem_limit_bytes=63 * 1024 * 1024
        ),
    )(
        queries, key_states, value_states, cotangent, norm_gains, tile_lists.T, clip_lengths
    )
    return pl.pallas_call(
        deliver,
        out_shape=(shaped, shaped, shaped, jax.ShapeDtypeStruct(norm_gains.shape, f32)),
        in_specs=[hbm] * 4,
        out_specs=(hbm,) * 4,
        scratch_shapes=[
            pltpu.VMEM((3, shard, width), bf), pltpu.VMEM((8, HEAD_DIM), f32), pltpu.VMEM(norm_gains.shape, f32),
            dma((3, PIECES)), dma((3, PIECES)), dma((2,)),
        ],
        compiler_params=pltpu.CompilerParams(vmem_limit_bytes=63 * 1024 * 1024),
    )(dq, dk, dv, gain_sum)


def solution(mesh):
    placed = (
        P("dp", "seq", None),
        P("dp", "seq", None),
        P("dp", "seq", None),
        P("dp", "seq", None),
        P(None, "dp"),
        P(),
        P("dp"),
    )
    return jax.shard_map(
        body,
        mesh=mesh,
        in_specs=placed,
        out_specs=(P("dp", "seq", None), P("dp", "seq", None), P("dp", "seq", None), P(None, "dp")),
        check_vma=False,
    )
```

time: 157 us -> 128 us (0.82)
  Pallas kernels: 148 us -> 127 us
  local copies, waits for them, and re-layouts: 7.56 us -> 0 us
    pallas_call x1 -> x2, Pallas kernels: 148 us -> 127 us  [the longest x1 124 us: body(): pl.pallas_call(functools.partial(kernel, (chips, shard, per_chip, cols, r...]
    unnamed x15 -> x0, local copies, waits for them, and re-layouts: 7.36 us -> none
where the time goes in v2:
time: 128 us
  Pallas kernels  127 us (99%)
  between operations  1.29 us (1%)
    pallas_call x1, Pallas kernels, body(): pl.pallas_call(functools.partial(kernel, (chips, shard, per_chip, cols, r...  124 us
    pallas_call x1, Pallas kernels, body(): pl.pallas_call(deliver, out_shape=(shaped, shaped, shaped, jax.ShapeDtype...  3.11 us

profile of v2, /device:TPU:1, one launch (start us, length us, event | category | flops | bytes accessed | tf_op | source)
XLA Modules:
  0.0 128.0 jit_solution(11323398677085007635)
XLA Ops:
  1.3 123.6 %shard_map.102 = (bf16[1,128,3072]{2,1,0:T(8,128)(2,1)}, bf16[1,128,3072]{2,1,0:T(8,128)(2,1)}, bf16[1,128,3072]{2,1,0:T(8,128)(2,1)}, f32[8,128]{1,0:T(8,128)}) custom-call(bf16[1,128,3072]{2,1,0:T(8,128)(2,1)} %q_in.1, bf16[1,128,3072]{2,1,0:T(8,128)(2,1)} %k_in.1, bf16[1,128,3072]{2,1,0:T(8,128)(2,1)} %v_in.1, bf16[1,128,128]{2,1,0:T(8,128)(2,1)} %c_in.1, ...), custom_call_target="tpu_custom_call" | custom-call | tf_op jit(solution)/shard_map/pallas_call | solution.py:483
  124.9 3.1 %shard_map.103 = (bf16[1,128,3072]{2,1,0:T(8,128)(2,1)}, bf16[1,128,3072]{2,1,0:T(8,128)(2,1)}, bf16[1,128,3072]{2,1,0:T(8,128)(2,1)}, f32[2,4]{1,0:T(2,128)}) custom-call(bf16[1,128,3072]{2,1,0:T(8,128)(2,1)} %get-tuple-element.8.q_ref, bf16[1,128,3072]{2,1,0:T(8,128)(2,1)} %get-tuple-element.9.k_ref, bf16[1,128,3072]{2,1,0:T(8,128)(2,1)} %get-tuple-element.10.v_ref, ...), custom_call_target="tpu_custom_call" | custom-call | tf_op jit(solution)/shard_map/pallas_call | solution.py:508

commit v3 on v2

--- a/solution.py
+++ b/solution.py
@@ -12,7 +12,6 @@
 
 HEAD_DIM = 128
 TILE = 64
-PIECES = 4
 EPS = 1e-06
 BLOCK = 256
 MESH = pl.DeviceIdType.MESH
@@ -54,7 +53,7 @@
     dq_out, dk_out, dv_out, gain_out,
     xq, xk, xv, cot, oq, ok, ov,
     qa, ka, kt, live, wbuf, gbuf, dk_acc, dv_acc,
-    gsrc, gx, gy, ysrc, gains, gacc, hz, hx, hy, hsrc, hsrc2,
+    gsrc, gx, gy, ysrc, gains, gacc, hz, hx, hy, hsrc, hsrc2, hsum,
     g_raw, lists, tsem,
     fsend, frecv, csend, crecv, osem, psem, rsend, orecv, gsend, grecv,
 ):
@@ -85,9 +84,62 @@
         return carry
 
     lax.fori_loop(1, 2 * chips, greet_seq, 0)
-    lax.fori_loop(1, cols, greet_col, 0)
-    lax.fori_loop(1, rows, greet_row, 0)
-    pl.semaphore_wait(barrier, 2 * chips - 1 + cols - 1 + rows - 1)
+
+    hub = 1
+    is_hub = seq == hub
+
+    @pl.when(is_hub)
+    def _():
+        lax.fori_loop(1, cols, greet_col, 0)
+        lax.fori_loop(1, rows, greet_row, 0)
+
+    for index, (source, landing) in enumerate(small):
+        pltpu.make_async_copy(source, landing, tsem.at[index]).wait()
+
+    lane = lax.broadcasted_iota(jnp.int32, (8, HEAD_DIM), 1)
+    sub = lax.broadcasted_iota(jnp.int32, (8, HEAD_DIM), 0)
+    owned = g_raw.shape[1]
+    spread = jnp.zeros((8, HEAD_DIM), jnp.float32)
+    for r in range(2):
+        for c in range(owned):
+            spot = jnp.logical_and(sub == r, lane == dp * owned + c)
+            spread = jnp.where(spot, g_raw[r, c], spread)
+    gsrc[...] = spread
+
+    @pl.when(is_hub)
+    def _():
+        pl.semaphore_wait(barrier, 2 * chips - 1 + cols - 1 + rows - 1)
+
+    @pl.when(seq != hub)
+    def _():
+        pl.semaphore_wait(barrier, 2 * chips - 1)
+
+    def send_gx(i, carry):
+        pltpu.make_async_remote_copy(
+            src_ref=gsrc, dst_ref=gx.at[col], send_sem=gsend.at[0], recv_sem=grecv.at[0],
+            device_id={"dp": row * cols + (col + i) % cols}, device_id_type=MESH,
+        ).start()
+        return carry
+
+    def send_gy(i, carry):
+        pltpu.make_async_remote_copy(
+            src_ref=ysrc, dst_ref=gy.at[row], send_sem=gsend.at[1], recv_sem=grecv.at[1],
+            device_id={"dp": (row + i) % rows * cols + col}, device_id_type=MESH,
+        ).start()
+        return carry
+
+    def send_gains(i, carry):
+        pltpu.make_async_remote_copy(
+            src_ref=gains, dst_ref=gains, send_sem=gsend.at[5], recv_sem=grecv.at[5],
+            device_id={"seq": (seq + i) % (2 * chips)}, device_id_type=MESH,
+        ).start()
+        return carry
+
+    @pl.when(is_hub)
+    def _():
+        lax.fori_loop(1, cols, send_gx, 0)
+        gx[col] = gsrc[...]
+
 
     arrays = ((q_in, xq), (k_in, xk), (v_in, xv))
     my_rows = pl.ds(pl.multiple_of(seq * shard, shard), shard)
@@ -156,24 +208,6 @@
     pass_on((chip - (last_step - 1) * way + chips) % chips, last_step, way, 0)
     remote(chips - 2, 0)
     at_home()
-    for which in range(1, per_chip):
-        remote, at_home = spread_head(which)
-        lax.fori_loop(0, chips - 1, remote, 0)
-        at_home()
-
-    for index, (source, landing) in enumerate(small):
-        pltpu.make_async_copy(source, landing, tsem.at[index]).wait()
-
-    lane = lax.broadcasted_iota(jnp.int32, (8, HEAD_DIM), 1)
-    sub = lax.broadcasted_iota(jnp.int32, (8, HEAD_DIM), 0)
-    owned = g_raw.shape[1]
-    spread = jnp.zeros((8, HEAD_DIM), jnp.float32)
-    for r in range(2):
-        for c in range(owned):
-            spot = jnp.logical_and(sub == r, lane == dp * owned + c)
-            spread = jnp.where(spot, g_raw[r, c], spread)
-    gsrc[...] = spread
-
     lanes = lax.broadcasted_iota(jnp.int32, (TILE, HEAD_DIM), 1)
     places = lax.broadcasted_iota(jnp.int32, (TILE, HEAD_DIM), 0)
     length = lengths[0]
@@ -195,20 +229,33 @@
         ka[here, HEAD_DIM:] = jnp.where(jnp.logical_or(mark, past), 1.0, 0.0).astype(jnp.bfloat16)
         return carry
 
-    lax.fori_loop(0, total // TILE, mask_tile, 0)
-    def send_gx(i, carry):
-        pltpu.make_async_remote_copy(
-            src_ref=gsrc, dst_ref=gx.at[col], send_sem=gsend.at[0], recv_sem=grecv.at[0],
-            device_id={"dp": row * cols + (col + i) % cols}, device_id_type=MESH,
-        ).start()
-        return carry
-
-    lax.fori_loop(1, cols, send_gx, 0)
-    gx[col] = gsrc[...]
-
+    tiles = total // TILE
+
+    @pl.when(is_hub)
+    def _():
+        wait_many(gx, cols - 1, grecv.at[0])
+        ysrc[...] = total_of(gx)
+
+    lax.fori_loop(0, tiles // 2, mask_tile, 0)
+
+    @pl.when(is_hub)
+    def _():
+        lax.fori_loop(1, rows, send_gy, 0)
+        gy[row] = ysrc[...]
+        wait_many(gy, rows - 1, grecv.at[1])
+        gains[...] = total_of(gy)
+
+    lax.fori_loop(tiles // 2, tiles, mask_tile, 0)
     gacc[...] = jnp.zeros_like(gacc)
-    wait_many(gx, cols - 1, grecv.at[0])
-    ysrc[...] = total_of(gx)
+
+    @pl.when(is_hub)
+    def _():
+        lax.fori_loop(1, 2 * chips, send_gains, 0)
+
+    for which in range(1, per_chip):
+        remote, at_home = spread_head(which)
+        lax.fori_loop(0, chips - 1, remote, 0)
+        at_home()
 
     passed(last_step, 0, crecv)
     own_cot.wait()
@@ -218,19 +265,12 @@
         device_id={"seq": partner}, device_id_type=MESH,
     )
     forward.start()
-    def send_gy(i, carry):
-        pltpu.make_async_remote_copy(
-            src_ref=ysrc, dst_ref=gy.at[row], send_sem=gsend.at[1], recv_sem=grecv.at[1],
-            device_id={"dp": (row + i) % rows * cols + col}, device_id_type=MESH,
-        ).start()
-        return carry
-
-    lax.fori_loop(1, rows, send_gy, 0)
-    gy[row] = ysrc[...]
-
-    wait_many(gy, rows - 1, grecv.at[1])
-    gains[...] = total_of(gy)
     forward.wait()
+
+    @pl.when(seq != hub)
+    def _():
+        wait_bytes(gains, grecv.at[5])
+
 
     def live_block(i, carry):
         tokens = i * BLOCK + lax.broadcasted_iota(jnp.int32, (BLOCK, HEAD_DIM), 0)
@@ -352,16 +392,12 @@
 
         lax.fori_loop(0, 2, back, 0)
 
-        @pl.when(slot == 1 - core)
+        @pl.when(jnp.logical_and(slot == 1 - core, seq != hub))
         def _():
-            def send_hz(i, carry):
-                pltpu.make_async_remote_copy(
-                    src_ref=hsrc, dst_ref=hz.at[seq], send_sem=gsend.at[2], recv_sem=grecv.at[2],
-                    device_id={"seq": (seq + i) % (2 * chips)}, device_id_type=MESH,
-                ).start()
-                return carry
-
-            lax.fori_loop(1, 2 * chips, send_hz, 0)
+            pltpu.make_async_remote_copy(
+                src_ref=hsrc, dst_ref=hz.at[seq], send_sem=gsend.at[2], recv_sem=grecv.at[2],
+                device_id={"seq": hub}, device_id_type=MESH,
+            ).start()
 
         lax.fori_loop(2, chips - 1, back, 0)
         give_back(chip, 1 - core, False)
@@ -370,10 +406,6 @@
 
     lax.fori_loop(0, 2 - core, one_head, 0)
 
-    wait_many(hz, 2 * chips - 1, grecv.at[2])
-    summed = total_of(hz)
-    hsrc2[0] = summed
-
     def send_hx(i, carry):
         pltpu.make_async_remote_copy(
             src_ref=hsrc2.at[0], dst_ref=hx.at[col], send_sem=gsend.at[3], recv_sem=grecv.at[3],
@@ -381,12 +413,6 @@
         ).start()
         return carry
 
-    lax.fori_loop(1, cols, send_hx, 0)
-    hx[col] = summed
-    wait_many(hx, cols - 1, grecv.at[3])
-    summed = total_of(hx)
-    hsrc2[1] = summed
-
     def send_hy(i, carry):
         pltpu.make_async_remote_copy(
             src_ref=hsrc2.at[1], dst_ref=hy.at[row], send_sem=gsend.at[4], recv_sem=grecv.at[4],
@@ -394,16 +420,42 @@
         ).start()
         return carry
 
-    lax.fori_loop(1, rows, send_hy, 0)
-    hy[row] = summed
-    wait_many(hy, rows - 1, grecv.at[4])
-    gain_out[...] = total_of(hy)
-
-    wait_many(gx, cols - 1, gsend.at[0])
-    wait_many(gy, rows - 1, gsend.at[1])
-    wait_many(hz, 2 * chips - 1, gsend.at[2])
-    wait_many(hx, cols - 1, gsend.at[3])
-    wait_many(hy, rows - 1, gsend.at[4])
+    def send_total(i, carry):
+        pltpu.make_async_remote_copy(
+            src_ref=hsum, dst_ref=hsum, send_sem=gsend.at[6], recv_sem=grecv.at[6],
+            device_id={"seq": (seq + i) % (2 * chips)}, device_id_type=MESH,
+        ).start()
+        return carry
+
+    @pl.when(is_hub)
+    def _():
+        wait_many(hz, 2 * chips - 1, grecv.at[2])
+        summed = total_of(hz)
+        hsrc2[0] = summed
+        hx[col] = summed
+        lax.fori_loop(1, cols, send_hx, 0)
+        wait_many(hx, cols - 1, grecv.at[3])
+        summed = total_of(hx)
+        hsrc2[1] = summed
+        hy[row] = summed
+        lax.fori_loop(1, rows, send_hy, 0)
+        wait_many(hy, rows - 1, grecv.at[4])
+        hsum[...] = total_of(hy)
+        lax.fori_loop(1, 2 * chips, send_total, 0)
+        wait_many(gx, cols - 1, gsend.at[0])
+        wait_many(gy, rows - 1, gsend.at[1])
+        wait_many(hx, cols - 1, gsend.at[3])
+        wait_many(hy, rows - 1, gsend.at[4])
+        wait_many(hz, 2 * chips - 1, gsend.at[5])
+        wait_many(hz, 2 * chips - 1, gsend.at[6])
+
+    @pl.when(seq != hub)
+    def _():
+        wait_bytes(hsrc, gsend.at[2])
+        wait_bytes(hsum, grecv.at[6])
+
+    gain_out[...] = hsum[...]
+
     for step in range(1, last_step):
         passed(step, 0, csend)
         passed(step, 1, csend)
@@ -428,37 +480,21 @@
         wait_bytes(out, orecv.at[index])
 
 
-def deliver(q_ref, k_ref, v_ref, gain_hbm, q_out, k_out, v_out, gain_out_hbm, held, gain_ref, gain_out, taken, given, gsem):
-    shard = q_ref.shape[1]
-    piece = shard // PIECES
-    pairs = ((q_ref, q_out), (k_ref, k_out), (v_ref, v_out))
-
-    def take(index, part):
-        span = pl.ds(part * piece, piece)
-        return pltpu.make_async_copy(pairs[index][0].at[0, span], held.at[index, span], taken.at[index, part])
-
-    def give(index, part):
-        span = pl.ds(part * piece, piece)
-        return pltpu.make_async_copy(held.at[index, span], pairs[index][1].at[0, span], given.at[index, part])
-
-    places = [(index, part) for index in range(3) for part in range(PIECES)]
-    gain_take = pltpu.make_async_copy(gain_hbm, gain_ref, gsem.at[0])
-    gain_give = pltpu.make_async_copy(gain_out, gain_out_hbm, gsem.at[1])
-    gain_take.start()
-    for place in places:
-        take(*place).start()
-    gain_take.wait()
+def deliver(q_ref, k_ref, v_ref, gain_ref, q_out, k_out, v_out, gain_hbm, gain_out, sems):
+    copies = [
+        pltpu.make_async_copy(source, out, sems.at[index])
+        for index, (source, out) in enumerate(((q_ref, q_out), (k_ref, k_out), (v_ref, v_out)))
+    ]
+    for copy in copies:
+        copy.start()
     owned = gain_out.shape[1]
     turned = pltpu.roll(gain_ref[...], HEAD_DIM - lax.axis_index("dp") * owned, 1)
-    count = lax.axis_size("dp") * lax.axis_size("seq") * shard * (q_ref.shape[2] // HEAD_DIM)
+    count = lax.axis_size("dp") * lax.axis_size("seq") * q_ref.shape[1] * (q_ref.shape[2] // HEAD_DIM)
     gain_out[...] = turned[:2, :owned] * (1.0 / math.sqrt(count))
-    for place in places:
-        take(*place).wait()
-        give(*place).start()
-    gain_give.start()
-    for place in places:
-        give(*place).wait()
-    gain_give.wait()
+    copies.append(pltpu.make_async_copy(gain_out, gain_hbm, sems.at[3]))
+    copies[3].start()
+    for copy in copies:
+        copy.wait()
 
 
 def body(queries, key_states, value_states, cotangent, norm_gains, tile_lists, clip_lengths):
@@ -480,11 +516,12 @@
     shaped = jax.ShapeDtypeStruct(queries.shape, bf)
     pair = pltpu.VMEM((2, total, HEAD_DIM), bf)
     tiny = lambda n: pltpu.VMEM((n, 8, HEAD_DIM), f32)
+    fixed = (queries, key_states, value_states, cotangent, norm_gains, tile_lists.T)
     dq, dk, dv, gain_sum = pl.pallas_call(
         functools.partial(kernel, (chips, shard, per_chip, cols, rows)),
         out_shape=(shaped, shaped, shaped, jax.ShapeDtypeStruct((8, HEAD_DIM), f32)),
         in_specs=[hbm] * 6 + [pl.BlockSpec(memory_space=pltpu.SMEM)],
-        out_specs=(hbm, hbm, hbm, vmem),
+        out_specs=(vmem, vmem, vmem, vmem),
         scratch_shapes=[
             pair, pair, pair, pltpu.VMEM((chips, 2, shard, HEAD_DIM), bf), pair, pair, pair,
             pltpu.VMEM((total, 2 * HEAD_DIM), bf), pltpu.VMEM((total, 2 * HEAD_DIM), bf),
@@ -494,27 +531,22 @@
             pltpu.VMEM((8, HEAD_DIM), f32), tiny(cols), tiny(rows), pltpu.VMEM((8, HEAD_DIM), f32),
             pltpu.VMEM((8, HEAD_DIM), f32),
             pltpu.VMEM((8, HEAD_DIM), f32), tiny(seq_count), tiny(cols), tiny(rows),
-            pltpu.VMEM((8, HEAD_DIM), f32), tiny(2),
+            pltpu.VMEM((8, HEAD_DIM), f32), tiny(2), pltpu.VMEM((8, HEAD_DIM), f32),
             pltpu.SMEM(norm_gains.shape, f32), pltpu.SMEM(tile_lists.T.shape, jnp.int32),
             dma((2,)),
-            dma((3,)), dma((2, 3)), dma((2, chips // 2)), dma((2, chips // 2)), dma(()), dma((2,)), dma((2, 3)), dma((3,)), dma((5,)), dma((5,)),
+            dma((3,)), dma((2, 3)), dma((2, chips // 2)), dma((2, chips // 2)), dma(()), dma((2,)), dma((2, 3)), dma((3,)), dma((7,)), dma((7,)),
         ],
         compiler_params=pltpu.CompilerParams(
-            collective_id=0, has_side_effects=True, vmem_limit_bytes=63 * 1024 * 1024
+            collective_id=0, has_side_effects=True, vmem_limit_bytes=32 * 1024 * 1024
         ),
-    )(
-        queries, key_states, value_states, cotangent, norm_gains, tile_lists.T, clip_lengths
-    )
+    )(*(pltpu.with_memory_space_constraint(x, pltpu.HBM) for x in fixed), clip_lengths)
     return pl.pallas_call(
         deliver,
         out_shape=(shaped, shaped, shaped, jax.ShapeDtypeStruct(norm_gains.shape, f32)),
-        in_specs=[hbm] * 4,
+        in_specs=[vmem] * 4,
         out_specs=(hbm,) * 4,
-        scratch_shapes=[
-            pltpu.VMEM((3, shard, width), bf), pltpu.VMEM((8, HEAD_DIM), f32), pltpu.VMEM(norm_gains.shape, f32),
-            dma((3, PIECES)), dma((3, PIECES)), dma((2,)),
-        ],
-        compiler_params=pltpu.CompilerParams(vmem_limit_bytes=63 * 1024 * 1024),
+        scratch_shapes=[pltpu.VMEM(norm_gains.shape, f32), dma((4,))],
+        compiler_params=pltpu.CompilerParams(vmem_limit_bytes=4 * 1024 * 1024),
     )(dq, dk, dv, gain_sum)
 
 

time: 128 us -> 122 us (0.953)
  Pallas kernels: 127 us -> 121 us
    pallas_call x1, Pallas kernels: 124 us -> 120 us  [body(): pl.pallas_call(functools.partial(kernel, (chips, shard, per_chip, cols, r...]
    pallas_call x1, Pallas kernels: 3.11 us -> 1.44 us  [body(): pl.pallas_call(deliver, out_shape=(shaped, shaped, shaped, jax.ShapeDtype...]
where the time goes in v3:
time: 122 us
  Pallas kernels  121 us (99%)
  between operations  1.29 us (1%)
    pallas_call x1, Pallas kernels, body(): pl.pallas_call(functools.partial(kernel, (chips, shard, per_chip, cols, r...  120 us

profile of v3, /device:TPU:1, one launch (start us, length us, event | category | flops | bytes accessed | tf_op | source)
XLA Modules:
  0.0 122.3 jit_solution(15276230587355818478)
XLA Ops:
  1.3 119.5 %shard_map.102 = (bf16[1,128,3072]{2,1,0:T(8,128)(2,1)S(1)}, bf16[1,128,3072]{2,1,0:T(8,128)(2,1)S(1)}, bf16[1,128,3072]{2,1,0:T(8,128)(2,1)S(1)}, f32[8,128]{1,0:T(8,128)S(1)}) custom-call(bf16[1,128,3072]{2,1,0:T(8,128)(2,1)} %q_in.1, bf16[1,128,3072]{2,1,0:T(8,128)(2,1)} %k_in.1, bf16[1,128,3072]{2,1,0:T(8,128)(2,1)} %v_in.1, bf16[1,128,128]{2,1,0:T(8,128)(2,1)} %c_in.1, ...), custom_call_target="tpu_custom_call" | custom-call | tf_op jit(solution)/shard_map/pallas_call | solution.py:520
  120.8 1.4 %shard_map.103 = (bf16[1,128,3072]{2,1,0:T(8,128)(2,1)}, bf16[1,128,3072]{2,1,0:T(8,128)(2,1)}, bf16[1,128,3072]{2,1,0:T(8,128)(2,1)}, f32[2,4]{1,0:T(2,128)}) custom-call(bf16[1,128,3072]{2,1,0:T(8,128)(2,1)S(1)} %get-tuple-element.8.q_ref, bf16[1,128,3072]{2,1,0:T(8,128)(2,1)S(1)} %get-tuple-element.9.k_ref, ...), custom_call_target="tpu_custom_call" | custom-call | tf_op jit(solution)/shard_map/pallas_call | solution.py:543

commit v4 on v3

--- a/solution.py
+++ b/solution.py
@@ -54,7 +54,7 @@
     xq, xk, xv, cot, oq, ok, ov,
     qa, ka, kt, live, wbuf, gbuf, dk_acc, dv_acc,
     gsrc, gx, gy, ysrc, gains, gacc, hz, hx, hy, hsrc, hsrc2, hsum,
-    g_raw, lists, tsem,
+    g_raw, lists, tsem, ahead, behind,
     fsend, frecv, csend, crecv, osem, psem, rsend, orecv, gsend, grecv,
 ):
     chips, shard, per_chip, cols, rows = sizes
@@ -71,9 +71,12 @@
 
     barrier = pltpu.get_barrier_semaphore()
 
-    def greet_seq(i, carry):
-        pl.semaphore_signal(barrier, inc=1, device_id={"seq": (seq + i) % (2 * chips)}, device_id_type=MESH)
-        return carry
+    after = 2 * ((chip + 1) % chips) + core
+    before = 2 * ((chip + chips - 1) % chips) + core
+    partner = 2 * chip + 1 - core
+
+    def tell(sem, target):
+        pl.semaphore_signal(sem, inc=1, device_id={"seq": target}, device_id_type=MESH)
 
     def greet_col(i, carry):
         pl.semaphore_signal(barrier, inc=1, device_id={"dp": row * cols + (col + i) % cols}, device_id_type=MESH)
@@ -83,7 +86,8 @@
         pl.semaphore_signal(barrier, inc=1, device_id={"dp": (row + i) % rows * cols + col}, device_id_type=MESH)
         return carry
 
-    lax.fori_loop(1, 2 * chips, greet_seq, 0)
+    for target in (after, before, partner):
+        tell(barrier, target)
 
     hub = 1
     is_hub = seq == hub
@@ -93,26 +97,13 @@
         lax.fori_loop(1, cols, greet_col, 0)
         lax.fori_loop(1, rows, greet_row, 0)
 
-    for index, (source, landing) in enumerate(small):
-        pltpu.make_async_copy(source, landing, tsem.at[index]).wait()
-
-    lane = lax.broadcasted_iota(jnp.int32, (8, HEAD_DIM), 1)
-    sub = lax.broadcasted_iota(jnp.int32, (8, HEAD_DIM), 0)
-    owned = g_raw.shape[1]
-    spread = jnp.zeros((8, HEAD_DIM), jnp.float32)
-    for r in range(2):
-        for c in range(owned):
-            spot = jnp.logical_and(sub == r, lane == dp * owned + c)
-            spread = jnp.where(spot, g_raw[r, c], spread)
-    gsrc[...] = spread
-
-    @pl.when(is_hub)
-    def _():
-        pl.semaphore_wait(barrier, 2 * chips - 1 + cols - 1 + rows - 1)
+    @pl.when(is_hub)
+    def _():
+        pl.semaphore_wait(barrier, 3 + cols - 1 + rows - 1)
 
     @pl.when(seq != hub)
     def _():
-        pl.semaphore_wait(barrier, 2 * chips - 1)
+        pl.semaphore_wait(barrier, 3)
 
     def send_gx(i, carry):
         pltpu.make_async_remote_copy(
@@ -134,12 +125,6 @@
             device_id={"seq": (seq + i) % (2 * chips)}, device_id_type=MESH,
         ).start()
         return carry
-
-    @pl.when(is_hub)
-    def _():
-        lax.fori_loop(1, cols, send_gx, 0)
-        gx[col] = gsrc[...]
-
 
     arrays = ((q_in, xq), (k_in, xk), (v_in, xv))
     my_rows = pl.ds(pl.multiple_of(seq * shard, shard), shard)
@@ -194,20 +179,49 @@
 
         return remote, at_home
 
+    def level(n):
+        if n > 1:
+            pl.semaphore_wait(ahead.at[n - 2], 1)
+            if n <= last_step:
+                pl.semaphore_wait(behind.at[n - 2], 1)
+        if n <= last_step:
+            tell(ahead.at[n - 1], before)
+        if n < last_step:
+            tell(behind.at[n - 1], after)
+
+    level(1)
     remote, at_home = spread_head(0)
     for step in range(1, last_step):
-        for side, way in ((0, 1), (1, -1)):
-            if step > 1:
+        if step == 1:
+            pass_on(chip, 1, 1, 0)
+            pass_on(chip, 1, -1, 1)
+        level(step + 1)
+        if step > 1:
+            for side, way in ((0, 1), (1, -1)):
                 passed(step - 1, side, crecv)
-            pass_on((chip - (step - 1) * way + chips) % chips, step, way, side)
+                pass_on((chip - (step - 1) * way + chips) % chips, step, way, side)
         remote(2 * step - 2, 0)
         remote(2 * step - 1, 0)
+    level(last_step + 1)
     for side in range(2):
         passed(last_step - 1, side, crecv)
     way = 1 - 2 * core
     pass_on((chip - (last_step - 1) * way + chips) % chips, last_step, way, 0)
     remote(chips - 2, 0)
     at_home()
+    for index, (source, landing) in enumerate(small):
+        pltpu.make_async_copy(source, landing, tsem.at[index]).wait()
+
+    lane = lax.broadcasted_iota(jnp.int32, (8, HEAD_DIM), 1)
+    sub = lax.broadcasted_iota(jnp.int32, (8, HEAD_DIM), 0)
+    owned = g_raw.shape[1]
+    spread = jnp.zeros((8, HEAD_DIM), jnp.float32)
+    for r in range(2):
+        for c in range(owned):
+            spot = jnp.logical_and(sub == r, lane == dp * owned + c)
+            spread = jnp.where(spot, g_raw[r, c], spread)
+    gsrc[...] = spread
+
     lanes = lax.broadcasted_iota(jnp.int32, (TILE, HEAD_DIM), 1)
     places = lax.broadcasted_iota(jnp.int32, (TILE, HEAD_DIM), 0)
     length = lengths[0]
@@ -230,13 +244,21 @@
         return carry
 
     tiles = total // TILE
+    lax.fori_loop(0, tiles // 4, mask_tile, 0)
+
+    @pl.when(is_hub)
+    def _():
+        lax.fori_loop(1, cols, send_gx, 0)
+        gx[col] = gsrc[...]
+
+    lax.fori_loop(tiles // 4, tiles // 2, mask_tile, 0)
 
     @pl.when(is_hub)
     def _():
         wait_many(gx, cols - 1, grecv.at[0])
         ysrc[...] = total_of(gx)
 
-    lax.fori_loop(0, tiles // 2, mask_tile, 0)
+    lax.fori_loop(tiles // 2, 3 * tiles // 4, mask_tile, 0)
 
     @pl.when(is_hub)
     def _():
@@ -245,7 +267,7 @@
         wait_many(gy, rows - 1, grecv.at[1])
         gains[...] = total_of(gy)
 
-    lax.fori_loop(tiles // 2, tiles, mask_tile, 0)
+    lax.fori_loop(3 * tiles // 4, tiles, mask_tile, 0)
     gacc[...] = jnp.zeros_like(gacc)
 
     @pl.when(is_hub)
@@ -259,7 +281,6 @@
 
     passed(last_step, 0, crecv)
     own_cot.wait()
-    partner = 2 * chip + 1 - core
     forward = pltpu.make_async_remote_copy(
         src_ref=cot.at[:, core], dst_ref=cot.at[:, core], send_sem=psem.at[0], recv_sem=psem.at[1],
         device_id={"seq": partner}, device_id_type=MESH,
@@ -533,7 +554,7 @@
             pltpu.VMEM((8, HEAD_DIM), f32), tiny(seq_count), tiny(cols), tiny(rows),
             pltpu.VMEM((8, HEAD_DIM), f32), tiny(2), pltpu.VMEM((8, HEAD_DIM), f32),
             pltpu.SMEM(norm_gains.shape, f32), pltpu.SMEM(tile_lists.T.shape, jnp.int32),
-            dma((2,)),
+            dma((2,)), pltpu.SemaphoreType.REGULAR((chips // 2,)), pltpu.SemaphoreType.REGULAR((chips // 2 - 1,)),
             dma((3,)), dma((2, 3)), dma((2, chips // 2)), dma((2, chips // 2)), dma(()), dma((2,)), dma((2, 3)), dma((3,)), dma((7,)), dma((7,)),
         ],
         compiler_params=pltpu.CompilerParams(

time: 122 us -> 121 us (level)
  Pallas kernels: 121 us -> 119 us
    pallas_call x1, Pallas kernels: 120 us -> 118 us  [body(): pl.pallas_call(functools.partial(kernel, (chips, shard, per_chip, cols, r...]
where the time goes in v4:
time: 121 us
  Pallas kernels  119 us (98%)
  between operations  1.29 us (1%)
    pallas_call x1, Pallas kernels, body(): pl.pallas_call(functools.partial(kernel, (chips, shard, per_chip, cols, r...  118 us

profile of v4, /device:TPU:1, one launch (start us, length us, event | category | flops | bytes accessed | tf_op | source)
XLA Modules:
  0.0 120.6 jit_solution(18081695681557145224)
XLA Ops:
  1.3 117.9 %shard_map.102 = (bf16[1,128,3072]{2,1,0:T(8,128)(2,1)S(1)}, bf16[1,128,3072]{2,1,0:T(8,128)(2,1)S(1)}, bf16[1,128,3072]{2,1,0:T(8,128)(2,1)S(1)}, f32[8,128]{1,0:T(8,128)S(1)}) custom-call(bf16[1,128,3072]{2,1,0:T(8,128)(2,1)} %q_in.1, bf16[1,128,3072]{2,1,0:T(8,128)(2,1)} %k_in.1, bf16[1,128,3072]{2,1,0:T(8,128)(2,1)} %v_in.1, bf16[1,128,128]{2,1,0:T(8,128)(2,1)} %c_in.1, ...), custom_call_target="tpu_custom_call" | custom-call | tf_op jit(solution)/shard_map/pallas_call | solution.py:541
  119.2 1.4 %shard_map.103 = (bf16[1,128,3072]{2,1,0:T(8,128)(2,1)}, bf16[1,128,3072]{2,1,0:T(8,128)(2,1)}, bf16[1,128,3072]{2,1,0:T(8,128)(2,1)}, f32[2,4]{1,0:T(2,128)}) custom-call(bf16[1,128,3072]{2,1,0:T(8,128)(2,1)S(1)} %get-tuple-element.8.q_ref, bf16[1,128,3072]{2,1,0:T(8,128)(2,1)S(1)} %get-tuple-element.9.k_ref, ...), custom_call_target="tpu_custom_call" | custom-call | tf_op jit(solution)/shard_map/pallas_call | solution.py:564

commit v5 on v4

--- a/solution.py
+++ b/solution.py
@@ -195,19 +195,36 @@
         if step == 1:
             pass_on(chip, 1, 1, 0)
             pass_on(chip, 1, -1, 1)
+        @pl.when(core == 0)
+        def _():
+            remote(2 * step - 2, 0)
+            remote(2 * step - 1, 0)
+
         level(step + 1)
         if step > 1:
             for side, way in ((0, 1), (1, -1)):
                 passed(step - 1, side, crecv)
                 pass_on((chip - (step - 1) * way + chips) % chips, step, way, side)
-        remote(2 * step - 2, 0)
-        remote(2 * step - 1, 0)
+
+        @pl.when(core == 1)
+        def _():
+            remote(2 * step - 2, 0)
+            remote(2 * step - 1, 0)
+
+    @pl.when(core == 0)
+    def _():
+        remote(chips - 2, 0)
+
     level(last_step + 1)
     for side in range(2):
         passed(last_step - 1, side, crecv)
     way = 1 - 2 * core
     pass_on((chip - (last_step - 1) * way + chips) % chips, last_step, way, 0)
-    remote(chips - 2, 0)
+
+    @pl.when(core == 1)
+    def _():
+        remote(chips - 2, 0)
+
     at_home()
     for index, (source, landing) in enumerate(small):
         pltpu.make_async_copy(source, landing, tsem.at[index]).wait()

time: 121 us -> 122 us (level)
  no operation moved by 1% of the time
where the time goes in v5:
time: 122 us; the launch traced here: 121 us
  Pallas kernels  120 us (98%)
  between operations  1.29 us (1%)
    pallas_call x1, Pallas kernels, body(): pl.pallas_call(functools.partial(kernel, (chips, shard, per_chip, cols, r...  119 us

profile of v5, /device:TPU:1, one launch (start us, length us, event | category | flops | bytes accessed | tf_op | source)
XLA Modules:
  0.0 121.5 jit_solution(2619450560487326285)
XLA Ops:
  1.3 118.8 %shard_map.102 = (bf16[1,128,3072]{2,1,0:T(8,128)(2,1)S(1)}, bf16[1,128,3072]{2,1,0:T(8,128)(2,1)S(1)}, bf16[1,128,3072]{2,1,0:T(8,128)(2,1)S(1)}, f32[8,128]{1,0:T(8,128)S(1)}) custom-call(bf16[1,128,3072]{2,1,0:T(8,128)(2,1)} %q_in.1, bf16[1,128,3072]{2,1,0:T(8,128)(2,1)} %k_in.1, bf16[1,128,3072]{2,1,0:T(8,128)(2,1)} %v_in.1, bf16[1,128,128]{2,1,0:T(8,128)(2,1)} %c_in.1, ...), custom_call_target="tpu_custom_call" | custom-call | tf_op jit(solution)/shard_map/pallas_call | solution.py:558
  120.1 1.4 %shard_map.103 = (bf16[1,128,3072]{2,1,0:T(8,128)(2,1)}, bf16[1,128,3072]{2,1,0:T(8,128)(2,1)}, bf16[1,128,3072]{2,1,0:T(8,128)(2,1)}, f32[2,4]{1,0:T(2,128)}) custom-call(bf16[1,128,3072]{2,1,0:T(8,128)(2,1)S(1)} %get-tuple-element.8.q_ref, bf16[1,128,3072]{2,1,0:T(8,128)(2,1)S(1)} %get-tuple-element.9.k_ref, ...), custom_call_target="tpu_custom_call" | custom-call | tf_op jit(solution)/shard_map/pallas_call | solution.py:581
